TPU v7x, 128 devices: a whole 4x4x4 slice. The times are simulated.
128 devices in a mesh: gx: 8 (over z, core), gy: 16 (over y, x).
Axes of the slice: x: 4, y: 4, z: 4, core: 2. Of those that a mesh axis runs over, the one named last changes fastest.
Arguments:
- fine_rhs: float32 [8, 16, 4, 32, 1024], P('gx', 'gy'), may hold values from -6 to 6
- fine_beta: float32 [8, 16, 4, 32, 1024], P('gx', 'gy'), may hold values from 0.5 to 5
- base_rhs: float32 [128, 256, 128], P('gx', 'gy'), may hold values from -6 to 6
- base_beta: float32 [128, 256, 128], P('gx', 'gy'), may hold values from 0.5 to 5
- slot_site: int32 [8, 16, 4], P('gx', 'gy'), may hold values from 0 to 7, as said below
- ghost_list: int32 [8, 16, 4, 6], P('gx', 'gy'), may hold values from -1 to 3, as said below
- box_count: int32 [8, 16], P('gx', 'gy'), may hold values from 1 to 4, as said below
Outputs:
- fine_solution: float32 [8, 16, 4, 32, 1024], P('gx', 'gy')
- base_solution: float32 [128, 256, 128], P('gx', 'gy')
Inputs may be any that keep to these rules, and one draw needn't show every extreme that they name: `slot_site`: the slots of one column name distinct sites. `box_count`: some column holds exactly 4 live boxes in every draw. `ghost_list`: for a live slot, entry d is the slot of the live box at the adjacent site across face d (same site in the column beside it for x and y faces, the site below or above in the same column for z faces), or -1 if there is none; all entries of slots that are not live are -1.
All inputs are finite; a program needn't handle non-finite values.
Results may differ from a plain program's by a relative error of at most 0.0003.
Values sent between devices are 32-bit elements; how exact they have to be, the bound alone decides.
A program may use at most 128 MiB of HBM per device.

v0:
```python
import jax
import jax.numpy as jnp
from jax import lax
from jax.sharding import PartitionSpec as P

CYCLES = 2
SWEEPS = 6


damping = 2.0 / 3.0


def with_halo(block, sides, width):
    for axis, dim in sides:
        count = lax.axis_size(axis)
        forward = [(i, i + 1) for i in range(count - 1)]
        backward = [(target, source) for source, target in forward]
        low = lax.ppermute(
            lax.slice_in_dim(block, block.shape[dim] - width, None, axis=dim), axis, forward
        )
        high = lax.ppermute(lax.slice_in_dim(block, 0, width, axis=dim), axis, backward)
        block = jnp.concatenate([low, block, high], axis=dim)
    return block


def from_behind(value, axis, steps):
    count = lax.axis_size(axis)
    first, last = (max(0, -steps), min(count, count - steps))
    return lax.ppermute(value, axis, [(source, source + steps) for source in range(first, last)])


def upsample(values, axis_list):
    for which_axis in axis_list:
        values = jnp.repeat(values, 2, axis=which_axis)
    return values


def shrink(values):
    size_x, size_y, size_z = values.shape
    blocks = values.reshape(size_x // 2, 2, size_y // 2, 2, size_z // 2, 2)
    return jnp.sum(blocks, axis=(1, 3, 5)) * 0.125


def level_apply(field, padded, coeffs, factor):
    nearby = padded[2:, 1:-1, 1:-1] + padded[:-2, 1:-1, 1:-1]
    nearby = nearby + padded[1:-1, 2:, 1:-1] + padded[1:-1, :-2, 1:-1]
    nearby = nearby + padded[1:-1, 1:-1, 2:] + padded[1:-1, 1:-1, :-2]
    return coeffs * factor * (6.0 * field - nearby)


def coarse_ghosts(halo_box, box_sites, extent):
    site_total = (halo_box.shape[2] - 2) // extent

    def from_plane(face_plane):
        slabs = jnp.take(face_plane.reshape(extent, site_total, extent), box_sites, axis=1)
        slabs = upsample(jnp.transpose(slabs, (1, 0, 2)), (1, 2))
        return slabs.reshape(slabs.shape[0], -1)

    column = halo_box[1:-1, 1:-1, :]

    def from_layer(layer_index):
        slabs = jnp.take(column, layer_index, axis=2)
        slabs = upsample(jnp.transpose(slabs, (2, 0, 1)), (1, 2))
        return slabs.reshape(slabs.shape[0], -1)

    return (
        from_plane(halo_box[0, 1:-1, 1:-1]),
        from_plane(halo_box[-1, 1:-1, 1:-1]),
        from_plane(halo_box[1:-1, 0, 1:-1]),
        from_plane(halo_box[1:-1, -1, 1:-1]),
        from_layer(box_sites * extent),
        from_layer((box_sites + 1) * extent + 1),
    )


def fine_faces(field):
    slot_total, fine_edge, face_area = field.shape
    return (
        field[:, 0, :],
        field[:, -1, :],
        field[:, :, :fine_edge].reshape(slot_total, face_area),
        field[:, :, face_area - fine_edge :].reshape(slot_total, face_area),
        field[:, :, 0::fine_edge].reshape(slot_total, face_area),
        field[:, :, fine_edge - 1 :: fine_edge].reshape(slot_total, face_area),
    )


def choose(received, link_index, fallback):
    picked = jnp.take(received, jnp.maximum(link_index, 0), axis=0)
    return jnp.where((link_index >= 0)[:, None], picked, fallback)


def assemble(face_set, from_west, from_east, from_south, from_north, coarse, link_table):
    return (
        choose(from_west, link_table[:, 0], coarse[0]),
        choose(from_east, link_table[:, 1], coarse[1]),
        choose(from_south, link_table[:, 2], coarse[2]),
        choose(from_north, link_table[:, 3], coarse[3]),
        choose(face_set[5], link_table[:, 4], coarse[4]),
        choose(face_set[4], link_table[:, 5], coarse[5]),
    )


def apply_fine(field, coeffs, layers):
    slot_total, fine_edge, face_area = field.shape
    depth_pos = jnp.arange(face_area) % fine_edge
    west_side = jnp.concatenate([layers[0][:, None, :], field[:, :-1, :]], axis=1)
    east_side = jnp.concatenate([field[:, 1:, :], layers[1][:, None, :]], axis=1)
    south_side = jnp.concatenate(
        [layers[2].reshape(slot_total, fine_edge, fine_edge), field[:, :, : face_area - fine_edge]],
        axis=2,
    )
    north_side = jnp.concatenate(
        [field[:, :, fine_edge:], layers[3].reshape(slot_total, fine_edge, fine_edge)], axis=2
    )
    zero_slab = jnp.zeros((slot_total, fine_edge, 1), field.dtype)
    lower_side = jnp.where(
        depth_pos == 0,
        jnp.repeat(layers[4].reshape(slot_total, fine_edge, fine_edge), fine_edge, axis=2),
        jnp.concatenate([zero_slab, field[:, :, :-1]], axis=2),
    )
    upper_side = jnp.where(
        depth_pos == fine_edge - 1,
        jnp.repeat(layers[5].reshape(slot_total, fine_edge, fine_edge), fine_edge, axis=2),
        jnp.concatenate([field[:, :, 1:], zero_slab], axis=2),
    )
    return coeffs * (
        6.0 * field - (west_side + east_side + south_side + north_side + lower_side + upper_side)
    )


def restrict_fine(field):
    slot_total, fine_edge, face_area = field.shape
    half_edge = fine_edge // 2
    blocks = field.reshape(slot_total, half_edge, 2, half_edge, 2, half_edge, 2)
    return jnp.sum(blocks, axis=(2, 4, 6)) * 0.125


def insert_blocks(coarse, blocks, box_sites, live_slots):
    extent = coarse.shape[0]
    site_total = coarse.shape[2] // extent
    slot_ids = jnp.arange(blocks.shape[0], dtype=jnp.int32)
    matches = (box_sites[None, :] == jnp.arange(site_total, dtype=jnp.int32)[:, None]) & live_slots[
        None, :
    ]
    owner = jnp.sum(jnp.where(matches, slot_ids[None, :] + 1, 0), axis=1) - 1
    picked = jnp.transpose(jnp.take(blocks, jnp.maximum(owner, 0), axis=0), (1, 2, 0, 3))
    stacked = coarse.reshape(extent, extent, site_total, extent)
    merged = jnp.where((owner >= 0)[None, None, :, None], picked, stacked)
    return merged.reshape(coarse.shape)


def prolong_fine(coarse, box_sites):
    extent = coarse.shape[0]
    site_total = coarse.shape[2] // extent
    slabs = jnp.take(coarse.reshape(extent, extent, site_total, extent), box_sites, axis=2)
    slabs = upsample(jnp.transpose(slabs, (2, 0, 1, 3)), (1, 2, 3))
    return slabs.reshape(slabs.shape[0], 2 * extent, -1)


def pad_depth(values):
    return jnp.pad(values, ((0, 0), (0, 0), (1, 1)))


def pad_solution(field):
    return pad_depth(with_halo(field, (("gx", 0), ("gy", 1)), 1))


def pad_correction(field):
    return pad_depth(with_halo(field, (("gx", 0), ("gy", 1)), 1))


def pad_coarsest(field):
    return pad_depth(with_halo(field, (("gx", 0), ("gy", 1)), 1))


def neighbour_faces(face_set):
    from_west = from_behind(face_set[1], "gx", 1)
    from_east = from_behind(face_set[0], "gx", -1)
    from_south = from_behind(face_set[3], "gy", 1)
    from_north = from_behind(face_set[2], "gy", -1)
    return (from_west, from_east, from_south, from_north)


def local(fine_rhs, fine_beta, base_rhs, base_beta, slot_site, ghost_list, box_count):
    rhs_fine = fine_rhs[0, 0]
    coeff_fine = fine_beta[0, 0]
    box_sites = slot_site[0, 0]
    link_table = ghost_list[0, 0]
    slot_total = rhs_fine.shape[0]
    extent = base_rhs.shape[0]
    live_slots = jnp.arange(slot_total, dtype=jnp.int32) < box_count[0, 0]
    keep_mask = live_slots.astype(jnp.float32)[:, None, None]
    coeff_levels = [base_beta]
    for level_index in range(3):
        coeff_levels.append(shrink(coeff_levels[-1]))
    factor_levels = [0.25 ** (level_index + 1) for level_index in range(4)]

    def multigrid(residual, level_index):
        coeffs = coeff_levels[level_index]
        factor = factor_levels[level_index]
        diagonal = 6.0 * coeffs * factor
        if level_index == 3:
            correction = damping * residual / diagonal
            for sweep_index in range(SWEEPS - 1):
                correction = (
                    correction
                    + damping
                    * (residual - level_apply(correction, pad_coarsest(correction), coeffs, factor))
                    / diagonal
                )
            return correction
        correction = damping * residual / diagonal
        leftover_part = residual - level_apply(
            correction, pad_correction(correction), coeffs, factor
        )
        correction = correction + upsample(
            multigrid(shrink(leftover_part), level_index + 1), (0, 1, 2)
        )
        return (
            correction
            + damping
            * (residual - level_apply(correction, pad_correction(correction), coeffs, factor))
            / diagonal
        )

    def ghost_layers(field, halo_box, received):
        face_set = fine_faces(field)
        received = neighbour_faces(face_set)
        from_west, from_east, from_south, from_north = received
        coarse = coarse_ghosts(halo_box, box_sites, extent)
        return assemble(face_set, from_west, from_east, from_south, from_north, coarse, link_table)

    def smooth(field, halo_box, received):
        layers = ghost_layers(field, halo_box, received)
        return (
            field
            + damping * (rhs_fine - apply_fine(field, coeff_fine, layers)) / (6.0 * coeff_fine)
        ) * keep_mask

    def prepare(base_values):
        return (pad_solution(base_values), None)

    fine_field = jnp.zeros_like(rhs_fine)
    base_field = jnp.zeros_like(base_rhs)
    for cycle_index in range(CYCLES):
        halo_box, received = prepare(base_field)
        fine_field = smooth(fine_field, halo_box, received)
        fine_left = rhs_fine - apply_fine(
            fine_field, coeff_fine, ghost_layers(fine_field, halo_box, None)
        )
        base_left = base_rhs - level_apply(base_field, halo_box, coeff_levels[0], factor_levels[0])
        base_left = insert_blocks(base_left, restrict_fine(fine_left), box_sites, live_slots)
        correction = multigrid(base_left, 0)
        base_field = base_field + correction
        fine_field = (fine_field + prolong_fine(correction, box_sites)) * keep_mask
        next_box, next_received = prepare(base_field)
        fine_field = smooth(fine_field, next_box, next_received)
        base_field = insert_blocks(base_field, restrict_fine(fine_field), box_sites, live_slots)
    return (fine_field[None, None], base_field)


def solution(mesh):
    return jax.shard_map(
        local,
        mesh=mesh,
        in_specs=(
            P("gx", "gy", None, None, None),
            P("gx", "gy", None, None, None),
            P("gx", "gy", None),
            P("gx", "gy", None),
            P("gx", "gy", None),
            P("gx", "gy", None, None),
            P("gx", "gy"),
        ),
        out_specs=(P("gx", "gy", None, None, None), P("gx", "gy", None)),
        check_vma=False,
    )
```

profile of v0, /device:TPU:56, one launch (start us, length us, event | category | flops | bytes accessed | tf_op | source)
XLA Modules:
  0.0 920.7 jit_solution(16147963868719358466)
XLA Ops:
  9.6 4.6 collective-permute-start.6
  34.7 6.0 collective-permute-start.7
  69.7 6.0 collective-permute-start.11
  99.4 8.3 copy.1792
  107.7 13.7 %reduce_sum.139 = f32[4,16,16,16]{0,3,2,1:T(8,128)} reduce(f32[4,16,2,16,2,16,2]{0,6,5,4,3,2,1:T(2,128)} %bitcast.325, f32[]{:T(128)} %constant.92.clone.1), dimensions={2,4,6}, to_apply=%region_1.5 | reduce | flops 114688 | bytes 589828 | tf_op jit(solution)/shard_map/reduce_sum | solution.py:136
  138.7 4.0 collective-permute-start.15
  142.7 9.7 %reshape.476 = f32[8,2,8,2,64,2]{5,4,3,2,1,0:T(8,128)} reshape(f32[16,16,128]{2,1,0:T(8,128)S(1)} %copy-done.2) | data formatting | bytes 262144 | tf_op jit(solution)/shard_map/reshape | solution.py:40
  152.4 4.0 reduce_sum.141
  156.9 9.7 %reshape.475 = f32[8,2,8,2,64,2]{5,4,3,2,1,0:T(8,128)} reshape(f32[16,16,128]{2,1,0:T(8,128)S(1)} %fusion.80) | data formatting | bytes 262144 | tf_op jit(solution)/shard_map/reshape | solution.py:40
  166.6 4.0 reduce_sum.140
  177.5 4.3 collective-permute-start.18
  183.7 5.7 collective-permute-done.19
  200.9 3.9 collective-permute-start.23
  204.9 3.7 collective-permute-done.23
  217.9 3.9 collective-permute-start.27
  221.8 3.6 collective-permute-done.27
  234.4 3.9 collective-permute-start.31
  238.4 3.6 collective-permute-done.31
  250.9 3.9 collective-permute-start.35
  254.9 3.6 collective-permute-done.35
  267.4 3.9 collective-permute-start.39
  271.4 3.6 collective-permute-done.39
  284.0 3.9 collective-permute-start.43
  287.9 3.6 collective-permute-done.43
  300.7 3.9 collective-permute-start.47
  304.7 3.7 collective-permute-done.47
  317.6 3.9 collective-permute-start.51
  321.6 3.7 collective-permute-done.51
  337.0 3.9 collective-permute-start.55
  340.9 3.7 collective-permute-done.55
  376.0 6.0 collective-permute-start.62
  384.1 6.2 collective-permute-start.63
  431.7 3.7 add_multiply_fusion.3
  435.4 8.3 copy.1832
  447.0 14.1 %reduce_sum.146 = f32[4,16,16,16]{0,3,2,1:T(8,128)} reduce(f32[4,16,2,16,2,16,2]{0,6,5,4,3,2,1:T(2,128)} %bitcast.324, f32[]{:T(128)} %constant.92.clone.1), dimensions={2,4,6}, to_apply=%region_8.14 | reduce | flops 114688 | bytes 589828 | tf_op jit(solution)/shard_map/reduce_sum | solution.py:136
  461.1 4.2 copy.1833
  486.3 6.0 collective-permute-start.70
  494.4 6.0 collective-permute-start.71
  562.4 3.9 collective-permute-start.74
  580.7 4.0 fusion.27
  584.7 9.2 copy.1878
  593.9 13.7 %reduce_sum.147 = f32[4,16,16,16]{0,3,2,1:T(8,128)} reduce(f32[4,16,2,16,2,16,2]{0,6,5,4,3,2,1:T(2,128)} %bitcast.326, f32[]{:T(128)} %constant.92.clone.1), dimensions={2,4,6}, to_apply=%region_9.15 | reduce | flops 114688 | bytes 589828 | tf_op jit(solution)/shard_map/reduce_sum | solution.py:136
  622.5 4.0 collective-permute-start.78
  628.5 5.7 collective-permute-done.79
  634.6 9.7 %reshape.538 = f32[8,2,8,2,64,2]{5,4,3,2,1,0:T(8,128)} reshape(f32[16,16,128]{2,1,0:T(8,128)S(1)} %fusion.59) | data formatting | bytes 262144 | tf_op jit(solution)/shard_map/reshape | solution.py:40
  644.3 4.0 reduce_sum.148
  657.1 4.1 collective-permute-start.83
  675.0 3.9 collective-permute-start.87
  679.0 3.7 collective-permute-done.87
  691.8 3.9 collective-permute-start.91
  708.3 3.9 collective-permute-start.95
  724.8 3.9 collective-permute-start.99
  741.3 3.9 collective-permute-start.103
  757.8 3.9 collective-permute-start.107
  774.6 3.9 collective-permute-start.111
  778.6 3.7 collective-permute-done.111
  791.5 3.9 collective-permute-start.115
  795.5 3.7 collective-permute-done.115
  810.9 3.9 collective-permute-start.119
  814.8 3.7 collective-permute-done.119
  844.1 6.0 collective-permute-start.126
  852.1 6.3 collective-permute-start.127
  892.3 8.3 copy.1918
  900.6 12.7 %reduce_sum.151 = f32[4,16,16,16]{0,3,2,1:T(8,128)S(1)} reduce(f32[4,16,2,16,2,16,2]{0,6,5,4,3,2,1:T(2,128)} %bitcast.327, f32[]{:T(128)} %constant.92.clone.1), dimensions={2,4,6}, to_apply=%region_13.19 | reduce | flops 114688 | bytes 589828 | tf_op jit(solution)/shard_map/reduce_sum | solution.py:136
  (1156 shorter events, 568.9 us)
Async XLA Ops:
  0.6 25.5 %collective-permute-start.1 = (f32[1,16,128]{2,1,0:T(8,128)S(1)}, f32[1,16,128]{2,1,0:T(8,128)S(1)}, u32[]{:S(2)}, u32[]{:S(2)}) collective-permute-start(f32[1,16,128]{2,1,0:T(8,128)S(1)} %broadcast.305), channel_id=1, source_target_pairs={{0,16},{16,32},{32,48},{48,64},{64,80},{80,96},{96,112},{1,17},{17... | collective-permute-start | bytes 24584 | tf_op jit(solution)/shard_map/ppermute | solution.py:18
  2.6 26.0 %collective-permute-start.3 = (f32[1,16,128]{2,1,0:T(8,128)S(1)}, f32[1,16,128]{2,1,0:T(8,128)S(1)}, u32[]{:S(2)}, u32[]{:S(2)}) collective-permute-start(f32[1,16,128]{2,1,0:T(8,128)S(1)} %broadcast.305), channel_id=1, source_target_pairs={{16,0},{32,16},{48,32},{64,48},{80,64},{96,80},{112,96},{17,1},{33... | collective-permute-start | bytes 24584 | tf_op jit(solution)/shard_map/ppermute | solution.py:21
  6.2 28.5 %collective-permute-start.4 = (f32[4,1024]{1,0:T(4,128)S(1)}, f32[4,1024]{1,0:T(4,128)S(1)}, u32[]{:S(2)}, u32[]{:S(2)}) collective-permute-start(f32[4,1024]{1,0:T(4,128)S(1)} %broadcast.304), channel_id=1, source_target_pairs={{0,1},{1,2},{2,3},{3,4},{4,5},{5,6},{6,7},{7,8},{8,9},{9,10},{10,1... | collective-permute-start | bytes 49160 | tf_op jit(solution)/shard_map/ppermute | solution.py:29
  9.6 31.7 %collective-permute-start.6 = (f32[4,1024]{1,0:T(4,128)S(1)}, f32[4,1024]{1,0:T(4,128)S(1)}, u32[]{:S(2)}, u32[]{:S(2)}) collective-permute-start(f32[4,1024]{1,0:T(4,128)S(1)} %broadcast.304), channel_id=1, source_target_pairs={{1,0},{2,1},{3,2},{4,3},{5,4},{6,5},{7,6},{8,7},{9,8},{10,9},{11,1... | collective-permute-start | bytes 49160 | tf_op jit(solution)/shard_map/ppermute | solution.py:29
  14.2 27.7 %collective-permute-start.2 = (f32[4,1024]{1,0:T(4,128)S(1)}, f32[4,1024]{1,0:T(4,128)S(1)}, u32[]{:S(2)}, u32[]{:S(2)}) collective-permute-start(f32[4,1024]{1,0:T(4,128)S(1)} %broadcast.304), channel_id=1, source_target_pairs={{16,0},{32,16},{48,32},{64,48},{80,64},{96,80},{112,96},{17,1},{33... | collective-permute-start | bytes 49160 | tf_op jit(solution)/shard_map/ppermute | solution.py:29
  26.1 17.0 %collective-permute-start = (f32[4,1024]{1,0:T(4,128)S(1)}, f32[4,1024]{1,0:T(4,128)S(1)}, u32[]{:S(2)}, u32[]{:S(2)}) collective-permute-start(f32[4,1024]{1,0:T(4,128)S(1)} %broadcast.304), channel_id=1, source_target_pairs={{0,16},{16,32},{32,48},{48,64},{64,80},{80,96},{96,112},{1,17},{17... | collective-permute-start | bytes 49160 | tf_op jit(solution)/shard_map/ppermute | solution.py:29
  28.6 15.7 %collective-permute-start.5 = (f32[18,1,128]{2,1,0:T(1,128)S(1)}, f32[18,1,128]{2,1,0:T(1,128)S(1)}, u32[]{:S(2)}, u32[]{:S(2)}) collective-permute-start(f32[18,1,128]{2,1,0:T(1,128)S(1)} %get-tuple-element.109), channel_id=1, source_target_pairs={{0,1},{1,2},{2,3},{3,4},{4,5},{5,6},{6,7},{7,8},{8,9},{9,10},{10,1... | collective-permute-start | bytes 27656 | tf_op jit(solution)/shard_map/ppermute | solution.py:18
  34.7 10.2 %collective-permute-start.7 = (f32[18,1,128]{2,1,0:T(1,128)S(1)}, f32[18,1,128]{2,1,0:T(1,128)S(1)}, u32[]{:S(2)}, u32[]{:S(2)}) collective-permute-start(f32[18,1,128]{2,1,0:T(1,128)S(1)} %get-tuple-element.110), channel_id=1, source_target_pairs={{1,0},{2,1},{3,2},{4,3},{5,4},{6,5},{7,6},{8,7},{9,8},{10,9},{11,1... | collective-permute-start | bytes 27656 | tf_op jit(solution)/shard_map/ppermute | solution.py:21
  67.6 25.1 %collective-permute-start.10 = (f32[4,1024]{1,0:T(4,128)S(1)}, f32[4,1024]{1,0:T(4,128)S(1)}, u32[]{:S(2)}, u32[]{:S(2)}) collective-permute-start(f32[4,1024]{1,0:T(4,128)S(1)} %reshape.462), channel_id=1, source_target_pairs={{0,1},{1,2},{2,3},{3,4},{4,5},{5,6},{6,7},{7,8},{8,9},{9,10},{10,1... | collective-permute-start | bytes 49160 | tf_op jit(solution)/shard_map/ppermute | solution.py:29
  69.7 23.9 %collective-permute-start.11 = (f32[4,1024]{1,0:T(4,128)S(1)}, f32[4,1024]{1,0:T(4,128)S(1)}, u32[]{:S(2)}, u32[]{:S(2)}) collective-permute-start(f32[4,1024]{1,0:T(4,128)S(1)} %reshape.464), channel_id=1, source_target_pairs={{1,0},{2,1},{3,2},{4,3},{5,4},{6,5},{7,6},{8,7},{9,8},{10,9},{11,1... | collective-permute-start | bytes 49160 | tf_op jit(solution)/shard_map/ppermute | solution.py:29
  75.7 18.6 %collective-permute-start.9 = (f32[4,1024]{1,0:T(4,128)S(1)}, f32[4,1024]{1,0:T(4,128)S(1)}, u32[]{:S(2)}, u32[]{:S(2)}) collective-permute-start(f32[4,1024]{1,0:T(4,128)S(1)} %get-tuple-element.93), channel_id=1, source_target_pairs={{16,0},{32,16},{48,32},{64,48},{80,64},{96,80},{112,96},{17,1},{33... | collective-permute-start | bytes 49160 | tf_op jit(solution)/shard_map/ppermute | solution.py:29
  77.8 17.6 %collective-permute-start.8 = (f32[4,1024]{1,0:T(4,128)S(1)}, f32[4,1024]{1,0:T(4,128)S(1)}, u32[]{:S(2)}, u32[]{:S(2)}) collective-permute-start(f32[4,1024]{1,0:T(4,128)S(1)} %get-tuple-element.94), channel_id=1, source_target_pairs={{0,16},{16,32},{32,48},{48,64},{64,80},{80,96},{96,112},{1,17},{17... | collective-permute-start | bytes 49160 | tf_op jit(solution)/shard_map/ppermute | solution.py:29
  136.5 20.0 %collective-permute-start.14 = (f32[18,1,128]{2,1,0:T(1,128)S(1)}, f32[18,1,128]{2,1,0:T(1,128)S(1)}, u32[]{:S(2)}, u32[]{:S(2)}) collective-permute-start(f32[18,1,128]{2,1,0:T(1,128)S(1)} %get-tuple-element.108), channel_id=1, source_target_pairs={{1,0},{2,1},{3,2},{4,3},{5,4},{6,5},{7,6},{8,7},{9,8},{10,9},{11,1... | collective-permute-start | bytes 27656 | tf_op jit(solution)/shard_map/ppermute | solution.py:21
  138.7 17.8 %collective-permute-start.15 = (f32[18,1,128]{2,1,0:T(1,128)S(1)}, f32[18,1,128]{2,1,0:T(1,128)S(1)}, u32[]{:S(2)}, u32[]{:S(2)}) collective-permute-start(f32[18,1,128]{2,1,0:T(1,128)S(1)} %get-tuple-element.107), channel_id=1, source_target_pairs={{0,1},{1,2},{2,3},{3,4},{4,5},{5,6},{6,7},{7,8},{8,9},{9,10},{10,1... | collective-permute-start | bytes 27656 | tf_op jit(solution)/shard_map/ppermute | solution.py:18
  177.5 6.2 collective-permute-start.18
  181.8 7.6 collective-permute-start.19
  200.9 7.6 collective-permute-start.23
  217.9 7.6 collective-permute-start.27
  234.4 7.6 collective-permute-start.31
  250.9 7.6 collective-permute-start.35
  267.4 7.6 collective-permute-start.39
  284.0 7.6 collective-permute-start.43
  300.7 7.6 collective-permute-start.47
  317.6 7.6 collective-permute-start.51
  337.0 7.7 collective-permute-start.55
  362.7 13.3 %collective-permute-start.57 = (f32[1,16,128]{2,1,0:T(8,128)S(1)}, f32[1,16,128]{2,1,0:T(8,128)S(1)}, u32[]{:S(2)}, u32[]{:S(2)}) collective-permute-start(f32[1,16,128]{2,1,0:T(8,128)S(1)} %get-tuple-element.117), channel_id=1, source_target_pairs={{0,16},{16,32},{32,48},{48,64},{64,80},{80,96},{96,112},{1,17},{17... | collective-permute-start | bytes 24584 | tf_op jit(solution)/shard_map/ppermute | solution.py:18
  364.6 17.4 %collective-permute-start.59 = (f32[1,16,128]{2,1,0:T(8,128)S(1)}, f32[1,16,128]{2,1,0:T(8,128)S(1)}, u32[]{:S(2)}, u32[]{:S(2)}) collective-permute-start(f32[1,16,128]{2,1,0:T(8,128)S(1)} %get-tuple-element.118), channel_id=1, source_target_pairs={{16,0},{32,16},{48,32},{64,48},{80,64},{96,80},{112,96},{17,1},{33... | collective-permute-start | bytes 24584 | tf_op jit(solution)/shard_map/ppermute | solution.py:21
  368.3 15.7 %collective-permute-start.56 = (f32[4,1024]{1,0:T(4,128)S(1)}, f32[4,1024]{1,0:T(4,128)S(1)}, u32[]{:S(2)}, u32[]{:S(2)}) collective-permute-start(f32[4,1024]{1,0:T(4,128)S(1)} %get-tuple-element.75), channel_id=1, source_target_pairs={{0,16},{16,32},{32,48},{48,64},{64,80},{80,96},{96,112},{1,17},{17... | collective-permute-start | bytes 49160 | tf_op jit(solution)/shard_map/ppermute | solution.py:29
  370.5 28.1 %collective-permute-start.58 = (f32[4,1024]{1,0:T(4,128)S(1)}, f32[4,1024]{1,0:T(4,128)S(1)}, u32[]{:S(2)}, u32[]{:S(2)}) collective-permute-start(f32[4,1024]{1,0:T(4,128)S(1)} %get-tuple-element.76), channel_id=1, source_target_pairs={{16,0},{32,16},{48,32},{64,48},{80,64},{96,80},{112,96},{17,1},{33... | collective-permute-start | bytes 49160 | tf_op jit(solution)/shard_map/ppermute | solution.py:29
  374.0 25.9 %collective-permute-start.60 = (f32[4,1024]{1,0:T(4,128)S(1)}, f32[4,1024]{1,0:T(4,128)S(1)}, u32[]{:S(2)}, u32[]{:S(2)}) collective-permute-start(f32[4,1024]{1,0:T(4,128)S(1)} %reshape.493), channel_id=1, source_target_pairs={{0,1},{1,2},{2,3},{3,4},{4,5},{5,6},{6,7},{7,8},{8,9},{9,10},{10,1... | collective-permute-start | bytes 49160 | tf_op jit(solution)/shard_map/ppermute | solution.py:29
  376.0 25.1 %collective-permute-start.62 = (f32[4,1024]{1,0:T(4,128)S(1)}, f32[4,1024]{1,0:T(4,128)S(1)}, u32[]{:S(2)}, u32[]{:S(2)}) collective-permute-start(f32[4,1024]{1,0:T(4,128)S(1)} %reshape.496), channel_id=1, source_target_pairs={{1,0},{2,1},{3,2},{4,3},{5,4},{6,5},{7,6},{8,7},{9,8},{10,9},{11,1... | collective-permute-start | bytes 49160 | tf_op jit(solution)/shard_map/ppermute | solution.py:29
  382.1 20.3 %collective-permute-start.61 = (f32[18,1,128]{2,1,0:T(1,128)S(1)}, f32[18,1,128]{2,1,0:T(1,128)S(1)}, u32[]{:S(2)}, u32[]{:S(2)}) collective-permute-start(f32[18,1,128]{2,1,0:T(1,128)S(1)} %get-tuple-element.103), channel_id=1, source_target_pairs={{0,1},{1,2},{2,3},{3,4},{4,5},{5,6},{6,7},{7,8},{8,9},{9,10},{10,1... | collective-permute-start | bytes 27656 | tf_op jit(solution)/shard_map/ppermute | solution.py:18
  384.1 18.4 %collective-permute-start.63 = (f32[18,1,128]{2,1,0:T(1,128)S(1)}, f32[18,1,128]{2,1,0:T(1,128)S(1)}, u32[]{:S(2)}, u32[]{:S(2)}) collective-permute-start(f32[18,1,128]{2,1,0:T(1,128)S(1)} %get-tuple-element.104), channel_id=1, source_target_pairs={{1,0},{2,1},{3,2},{4,3},{5,4},{6,5},{7,6},{8,7},{9,8},{10,9},{11,1... | collective-permute-start | bytes 27656 | tf_op jit(solution)/shard_map/ppermute | solution.py:21
  470.7 15.6 %collective-permute-start.65 = (f32[1,16,128]{2,1,0:T(8,128)S(1)}, f32[1,16,128]{2,1,0:T(8,128)S(1)}, u32[]{:S(2)}, u32[]{:S(2)}) collective-permute-start(f32[1,16,128]{2,1,0:T(8,128)S(1)} %slice.1458), channel_id=1, source_target_pairs={{0,16},{16,32},{32,48},{48,64},{64,80},{80,96},{96,112},{1,17},{17... | collective-permute-start | bytes 24584 | tf_op jit(solution)/shard_map/ppermute | solution.py:18
  474.9 17.5 %collective-permute-start.67 = (f32[1,16,128]{2,1,0:T(8,128)S(1)}, f32[1,16,128]{2,1,0:T(8,128)S(1)}, u32[]{:S(2)}, u32[]{:S(2)}) collective-permute-start(f32[1,16,128]{2,1,0:T(8,128)S(1)} %slice.1463), channel_id=1, source_target_pairs={{16,0},{32,16},{48,32},{64,48},{80,64},{96,80},{112,96},{17,1},{33... | collective-permute-start | bytes 24584 | tf_op jit(solution)/shard_map/ppermute | solution.py:21
  478.6 15.8 %collective-permute-start.64 = (f32[4,1024]{1,0:T(4,128)S(1)}, f32[4,1024]{1,0:T(4,128)S(1)}, u32[]{:S(2)}, u32[]{:S(2)}) collective-permute-start(f32[4,1024]{1,0:T(4,128)S(1)} %get-tuple-element.65), channel_id=1, source_target_pairs={{0,16},{16,32},{32,48},{48,64},{64,80},{80,96},{96,112},{1,17},{17... | collective-permute-start | bytes 49160 | tf_op jit(solution)/shard_map/ppermute | solution.py:29
  480.8 28.0 %collective-permute-start.66 = (f32[4,1024]{1,0:T(4,128)S(1)}, f32[4,1024]{1,0:T(4,128)S(1)}, u32[]{:S(2)}, u32[]{:S(2)}) collective-permute-start(f32[4,1024]{1,0:T(4,128)S(1)} %get-tuple-element.66), channel_id=1, source_target_pairs={{16,0},{32,16},{48,32},{64,48},{80,64},{96,80},{112,96},{17,1},{33... | collective-permute-start | bytes 49160 | tf_op jit(solution)/shard_map/ppermute | solution.py:29
  484.3 25.8 %collective-permute-start.68 = (f32[4,1024]{1,0:T(4,128)S(1)}, f32[4,1024]{1,0:T(4,128)S(1)}, u32[]{:S(2)}, u32[]{:S(2)}) collective-permute-start(f32[4,1024]{1,0:T(4,128)S(1)} %reshape.510), channel_id=1, source_target_pairs={{0,1},{1,2},{2,3},{3,4},{4,5},{5,6},{6,7},{7,8},{8,9},{9,10},{10,1... | collective-permute-start | bytes 49160 | tf_op jit(solution)/shard_map/ppermute | solution.py:29
  486.3 25.0 %collective-permute-start.70 = (f32[4,1024]{1,0:T(4,128)S(1)}, f32[4,1024]{1,0:T(4,128)S(1)}, u32[]{:S(2)}, u32[]{:S(2)}) collective-permute-start(f32[4,1024]{1,0:T(4,128)S(1)} %reshape.514), channel_id=1, source_target_pairs={{1,0},{2,1},{3,2},{4,3},{5,4},{6,5},{7,6},{8,7},{9,8},{10,9},{11,1... | collective-permute-start | bytes 49160 | tf_op jit(solution)/shard_map/ppermute | solution.py:29
  492.5 20.1 %collective-permute-start.69 = (f32[18,1,128]{2,1,0:T(1,128)S(1)}, f32[18,1,128]{2,1,0:T(1,128)S(1)}, u32[]{:S(2)}, u32[]{:S(2)}) collective-permute-start(f32[18,1,128]{2,1,0:T(1,128)S(1)} %get-tuple-element.101), channel_id=1, source_target_pairs={{0,1},{1,2},{2,3},{3,4},{4,5},{5,6},{6,7},{7,8},{8,9},{9,10},{10,1... | collective-permute-start | bytes 27656 | tf_op jit(solution)/shard_map/ppermute | solution.py:18
  494.4 18.2 %collective-permute-start.71 = (f32[18,1,128]{2,1,0:T(1,128)S(1)}, f32[18,1,128]{2,1,0:T(1,128)S(1)}, u32[]{:S(2)}, u32[]{:S(2)}) collective-permute-start(f32[18,1,128]{2,1,0:T(1,128)S(1)} %get-tuple-element.102), channel_id=1, source_target_pairs={{1,0},{2,1},{3,2},{4,3},{5,4},{6,5},{7,6},{8,7},{9,8},{10,9},{11,1... | collective-permute-start | bytes 27656 | tf_op jit(solution)/shard_map/ppermute | solution.py:21
  558.9 15.8 %collective-permute-start.75 = (f32[4,1024]{1,0:T(4,128)}, f32[4,1024]{1,0:T(4,128)S(1)}, u32[]{:S(2)}, u32[]{:S(2)}) collective-permute-start(f32[4,1024]{1,0:T(4,128)} %reshape.527), channel_id=1, source_target_pairs={{1,0},{2,1},{3,2},{4,3},{5,4},{6,5},{7,6},{8,7},{9,8},{10,9},{11,1... | collective-permute-start | bytes 49160 | tf_op jit(solution)/shard_map/ppermute | solution.py:29
  562.4 13.8 %collective-permute-start.74 = (f32[4,1024]{1,0:T(4,128)}, f32[4,1024]{1,0:T(4,128)S(1)}, u32[]{:S(2)}, u32[]{:S(2)}) collective-permute-start(f32[4,1024]{1,0:T(4,128)} %reshape.525), channel_id=1, source_target_pairs={{0,1},{1,2},{2,3},{3,4},{4,5},{5,6},{6,7},{7,8},{8,9},{9,10},{10,1... | collective-permute-start | bytes 49160 | tf_op jit(solution)/shard_map/ppermute | solution.py:29
  566.3 11.3 %collective-permute-start.73 = (f32[4,1024]{1,0:T(4,128)}, f32[4,1024]{1,0:T(4,128)S(1)}, u32[]{:S(2)}, u32[]{:S(2)}) collective-permute-start(f32[4,1024]{1,0:T(4,128)} %get-tuple-element.63), channel_id=1, source_target_pairs={{16,0},{32,16},{48,32},{64,48},{80,64},{96,80},{112,96},{17,1},{33... | collective-permute-start | bytes 49160 | tf_op jit(solution)/shard_map/ppermute | solution.py:29
  568.2 11.0 %collective-permute-start.72 = (f32[4,1024]{1,0:T(4,128)}, f32[4,1024]{1,0:T(4,128)S(1)}, u32[]{:S(2)}, u32[]{:S(2)}) collective-permute-start(f32[4,1024]{1,0:T(4,128)} %get-tuple-element.64), channel_id=1, source_target_pairs={{0,16},{16,32},{32,48},{48,64},{64,80},{80,96},{96,112},{1,17},{17... | collective-permute-start | bytes 49160 | tf_op jit(solution)/shard_map/ppermute | solution.py:29
  626.5 7.7 collective-permute-start.79
  657.1 7.6 collective-permute-start.83
  675.0 7.6 collective-permute-start.87
  691.8 7.6 collective-permute-start.91
  708.3 7.6 collective-permute-start.95
  724.8 7.6 collective-permute-start.99
  741.3 7.6 collective-permute-start.103
  757.8 7.6 collective-permute-start.107
  774.6 7.6 collective-permute-start.111
  791.5 7.6 collective-permute-start.115
  810.9 7.7 collective-permute-start.119
  830.8 13.3 %collective-permute-start.121 = (f32[1,16,128]{2,1,0:T(8,128)S(1)}, f32[1,16,128]{2,1,0:T(8,128)S(1)}, u32[]{:S(2)}, u32[]{:S(2)}) collective-permute-start(f32[1,16,128]{2,1,0:T(8,128)S(1)} %get-tuple-element.111), channel_id=1, source_target_pairs={{0,16},{16,32},{32,48},{48,64},{64,80},{80,96},{96,112},{1,17},{17... | collective-permute-start | bytes 24584 | tf_op jit(solution)/shard_map/ppermute | solution.py:18
  832.7 17.4 %collective-permute-start.123 = (f32[1,16,128]{2,1,0:T(8,128)S(1)}, f32[1,16,128]{2,1,0:T(8,128)S(1)}, u32[]{:S(2)}, u32[]{:S(2)}) collective-permute-start(f32[1,16,128]{2,1,0:T(8,128)S(1)} %get-tuple-element.112), channel_id=1, source_target_pairs={{16,0},{32,16},{48,32},{64,48},{80,64},{96,80},{112,96},{17,1},{33... | collective-permute-start | bytes 24584 | tf_op jit(solution)/shard_map/ppermute | solution.py:21
  836.4 15.7 %collective-permute-start.120 = (f32[4,1024]{1,0:T(4,128)S(1)}, f32[4,1024]{1,0:T(4,128)S(1)}, u32[]{:S(2)}, u32[]{:S(2)}) collective-permute-start(f32[4,1024]{1,0:T(4,128)S(1)} %get-tuple-element.45), channel_id=1, source_target_pairs={{0,16},{16,32},{32,48},{48,64},{64,80},{80,96},{96,112},{1,17},{17... | collective-permute-start | bytes 49160 | tf_op jit(solution)/shard_map/ppermute | solution.py:29
  838.6 27.7 %collective-permute-start.122 = (f32[4,1024]{1,0:T(4,128)S(1)}, f32[4,1024]{1,0:T(4,128)S(1)}, u32[]{:S(2)}, u32[]{:S(2)}) collective-permute-start(f32[4,1024]{1,0:T(4,128)S(1)} %get-tuple-element.46), channel_id=1, source_target_pairs={{16,0},{32,16},{48,32},{64,48},{80,64},{96,80},{112,96},{17,1},{33... | collective-permute-start | bytes 49160 | tf_op jit(solution)/shard_map/ppermute | solution.py:29
  842.1 24.9 %collective-permute-start.124 = (f32[4,1024]{1,0:T(4,128)S(1)}, f32[4,1024]{1,0:T(4,128)S(1)}, u32[]{:S(2)}, u32[]{:S(2)}) collective-permute-start(f32[4,1024]{1,0:T(4,128)S(1)} %reshape.555), channel_id=1, source_target_pairs={{0,1},{1,2},{2,3},{3,4},{4,5},{5,6},{6,7},{7,8},{8,9},{9,10},{10,1... | collective-permute-start | bytes 49160 | tf_op jit(solution)/shard_map/ppermute | solution.py:29
  844.1 23.6 %collective-permute-start.126 = (f32[4,1024]{1,0:T(4,128)S(1)}, f32[4,1024]{1,0:T(4,128)S(1)}, u32[]{:S(2)}, u32[]{:S(2)}) collective-permute-start(f32[4,1024]{1,0:T(4,128)S(1)} %reshape.558), channel_id=1, source_target_pairs={{1,0},{2,1},{3,2},{4,3},{5,4},{6,5},{7,6},{8,7},{9,8},{10,9},{11,1... | collective-permute-start | bytes 49160 | tf_op jit(solution)/shard_map/ppermute | solution.py:29
  850.2 18.2 %collective-permute-start.125 = (f32[18,1,128]{2,1,0:T(1,128)S(1)}, f32[18,1,128]{2,1,0:T(1,128)S(1)}, u32[]{:S(2)}, u32[]{:S(2)}) collective-permute-start(f32[18,1,128]{2,1,0:T(1,128)S(1)} %get-tuple-element.95), channel_id=1, source_target_pairs={{0,1},{1,2},{2,3},{3,4},{4,5},{5,6},{6,7},{7,8},{8,9},{9,10},{10,1... | collective-permute-start | bytes 27656 | tf_op jit(solution)/shard_map/ppermute | solution.py:18
  852.1 16.3 %collective-permute-start.127 = (f32[18,1,128]{2,1,0:T(1,128)S(1)}, f32[18,1,128]{2,1,0:T(1,128)S(1)}, u32[]{:S(2)}, u32[]{:S(2)}) collective-permute-start(f32[18,1,128]{2,1,0:T(1,128)S(1)} %get-tuple-element.96), channel_id=1, source_target_pairs={{1,0},{2,1},{3,2},{4,3},{5,4},{6,5},{7,6},{8,7},{9,8},{10,9},{11,1... | collective-permute-start | bytes 27656 | tf_op jit(solution)/shard_map/ppermute | solution.py:21
  (205 other events, 1475.4 us)
where the time goes:
time: 935 us; the launch traced here: 921 us
  starting transfers between devices  357 us (38%)
  local copies, waits for them, and re-layouts  299 us (32%)
  waiting for transfers between devices  136 us (15%)
  other arithmetic  122 us (13%)
    ppermute x52, starting transfers between devices, with_halo(): lax.ppermute(lax.slice_in_dim(block, block.shape[dim] - width, None, axis...  150 us
    ppermute x52, waiting for transfers between devices, with_halo(): lax.ppermute(lax.slice_in_dim(block, block.shape[dim] - width, None, axis...  136 us
    ppermute x52, starting transfers between devices, with_halo(): lax.ppermute(lax.slice_in_dim(block, 0, width, axis=dim), axis, backward)  131 us
    ppermute x24, starting transfers between devices, from_behind(): lax.ppermute(value, axis, [(source, source + steps) for source in range(f...  75.4 us
    reduce_sum x4, other arithmetic, restrict_fine(): return jnp.sum(blocks, axis=(2, 4, 6)) * 0.125  54 us
    gather x36, local copies, waits for them, and re-layouts, choose(): picked = jnp.take(received, jnp.maximum(link_index, 0), axis=0)  32.9 us
    reshape x7, local copies, waits for them, and re-layouts, shrink(): blocks = values.reshape(size_x // 2, 2, size_y // 2, 2, size_z // 2, 2)  31.5 us
  transfers between devices with their start and end apart: 128, of which 43 were waited for; matrix products, arithmetic and copies ran while one was open for 10% of the time, Pallas kernels for 0%

commit v1 on v0

v1 whole, which is shorter than its diff:
```python
import jax
import jax.numpy as jnp
from jax import lax
from jax.experimental import pallas as pl
from jax.experimental.pallas import tpu as pltpu
from jax.sharding import PartitionSpec as P

CYCLES = 2
SWEEPS = 6
MESH = pl.DeviceIdType.MESH
F32 = jnp.float32

S0, O0 = 24, 4
S1, O1 = 24, 8
S2, O2 = 8, 2

DIRS = ((-1, 0), (1, 0), (0, -1), (0, 1), (-1, -1), (-1, 1), (1, -1), (1, 1))
REACH = (-3, -2, -1, 1, 2, 3)
PARTNERS = DIRS + tuple((0, k) for k in (-3, -2, 2, 3)) + tuple((k, 0) for k in (-3, -2, 2, 3))

SEM_COUNT = 8 + 4 + 2 * (4 + 8 + 8 + 6 + 6)


def roll(value, shift, axis):
    return pltpu.roll(value, shift % value.shape[axis], axis)


def tile(value, count):
    return value if count == 1 else jnp.concatenate([value] * count, axis=0)


def pick(value, index):
    parts = [
        jnp.take_along_axis(value[k : k + 8], index, axis=1, mode="promise_in_bounds")
        for k in range(0, value.shape[0], 8)
    ]
    return parts[0] if len(parts) == 1 else jnp.concatenate(parts, axis=0)


def kernel(
    nx,
    ny,
    site_ref,
    link_ref,
    count_ref,
    frhs_ref,
    fbeta_ref,
    brhs_ref,
    bbeta_ref,
    fout_ref,
    bout_ref,
    FA,
    FB,
    G,
    BT,
    PC,
    CGZ,
    T,
    GX,
    CB,
    B0,
    BR,
    C0,
    W0,
    P0,
    E0,
    T0,
    C1,
    W1,
    P1,
    E1,
    U1,
    T1,
    C2,
    W2,
    P2,
    E2,
    T2,
    W3,
    SP,
    RP,
    SA,
    RA,
    SB,
    RB,
    SC,
    SCC,
    RC,
    RCC,
    SD,
    RD,
    SW,
    RW,
    SX,
    RX,
    send_sem,
    recv_sem,
):
    gx = lax.axis_index("gx")
    gy = lax.axis_index("gy")
    counter = [0]
    pending = []

    def inside(dx, dy):
        conds = []
        if dx < 0:
            conds.append(gx >= -dx)
        if dx > 0:
            conds.append(gx < nx - dx)
        if dy < 0:
            conds.append(gy >= -dy)
        if dy > 0:
            conds.append(gy < ny - dy)
        out = conds[0]
        for cond in conds[1:]:
            out = jnp.logical_and(out, cond)
        return out

    def start(messages):
        sent = []
        for dx, dy, source, target in messages:
            k = counter[0]
            counter[0] += 1

            def copy(dx=dx, dy=dy, source=source, target=target, k=k):
                return pltpu.make_async_remote_copy(
                    src_ref=source,
                    dst_ref=target,
                    send_sem=send_sem.at[k],
                    recv_sem=recv_sem.at[k],
                    device_id=(gx + dx, gy + dy),
                    device_id_type=MESH,
                )

            pl.when(inside(dx, dy))(lambda copy=copy: copy().start())
            sent.append((dx, dy, copy))
        pending.extend(sent)
        return sent

    def finish(sent):
        for dx, dy, copy in sent:
            pl.when(inside(-dx, -dy))(lambda copy=copy: copy().wait_recv())

    for ref in (B0, BR, C0, W0, P0, E0, C1, P1, E1, U1, FA, FB, GX, CB, SCC, RX):
        ref[...] = jnp.zeros(ref.shape, F32)
    for ref in (RP, RA, RB, RC, RCC, RD, RW):
        ref[...] = jnp.zeros(ref.shape, F32)

    barrier = pltpu.get_barrier_semaphore()
    total = jnp.int32(0)
    for dx, dy in PARTNERS:
        there = inside(dx, dy)

        def greet(dx=dx, dy=dy):
            pl.semaphore_signal(barrier, inc=1, device_id=(gx + dx, gy + dy), device_id_type=MESH)

        pl.when(there)(greet)
        total = total + there.astype(jnp.int32)

    lane = lax.broadcasted_iota(jnp.int32, (8, 128), 1)
    row8 = lax.broadcasted_iota(jnp.int32, (8, 128), 0)
    slot = lane >> 5
    zf = lane & 31
    sites = [site_ref[0, 0, s] for s in range(4)]
    count = count_ref[0, 0]

    def by_slot(values):
        out = jnp.full((8, 128), values[3], jnp.int32)
        for s in (2, 1, 0):
            out = jnp.where(slot == s, values[s], out)
        return out

    site_v = by_slot(sites)
    links = [by_slot([link_ref[0, 0, s, d] for s in range(4)]) for d in range(6)]
    keep8 = jnp.where(slot < count, 1.0, 0.0).astype(F32)
    index_low = jnp.where(zf == 0, jnp.maximum(links[4], 0) * 32 + 31, jnp.maximum(lane - 1, 0))
    index_high = jnp.where(zf == 31, jnp.maximum(links[5], 0) * 32, jnp.minimum(lane + 1, 127))
    mask_low = jnp.where((zf > 0) | (links[4] >= 0), 1.0, 0.0).astype(F32)
    mask_high = jnp.where((zf < 31) | (links[5] >= 0), 1.0, 0.0).astype(F32)
    index_p = site_v * 16 + (zf >> 1)
    index_cz = jnp.where(zf < 16, jnp.maximum(site_v * 16 - 1, 0), jnp.minimum(site_v * 16 + 16, 127))
    mask_cz = jnp.where(
        ((zf == 0) & (links[4] < 0) & (site_v > 0)) | ((zf == 31) & (links[5] < 0) & (site_v < 7)), 1.0, 0.0
    ).astype(F32)
    index_g = [jnp.maximum(links[d], 0) * 32 + zf for d in range(4)]
    mask_g = [jnp.where(links[d] >= 0, 1.0, 0.0).astype(F32) for d in range(4)]
    index_in = jnp.zeros((8, 128), jnp.int32)
    mask_in = jnp.zeros((8, 128), F32)
    for s in range(4):
        held = ((lane >> 4) == sites[s]) & (count > s)
        index_in = jnp.where(held, s * 32 + 2 * (lane & 15), index_in)
        mask_in = jnp.where(held, 1.0, mask_in)
    keep32 = tile(keep8, 4)
    mask_low32 = tile(mask_low, 4)
    mask_high32 = tile(mask_high, 4)
    mask_in16 = tile(mask_in, 2)
    row32 = lax.broadcasted_iota(jnp.int32, (32, 128), 0)
    first32 = jnp.where(row32 == 0, 1.0, 0.0).astype(F32)
    last32 = jnp.where(row32 == 31, 1.0, 0.0).astype(F32)

    lane32 = lax.broadcasted_iota(jnp.int32, (32, 128), 1)
    bit0 = ((lane32 >> 5) & 1) == 0
    bit1 = ((lane32 >> 6) & 1) == 0

    def swap(a, b, bit, shift):
        return jnp.where(bit, a, roll(b, shift, 1)), jnp.where(bit, roll(a, -shift, 1), b)

    def exchange_chunks(parts):
        a, b = swap(parts[0], parts[1], bit0, 32)
        c, d = swap(parts[2], parts[3], bit0, 32)
        a, c = swap(a, c, bit1, 64)
        b, d = swap(b, d, bit1, 64)
        return a, b, c, d

    def load_fine(j, _):
        lanes = pl.ds(pl.multiple_of(j * 128, 128), 128)
        betas = exchange_chunks([fbeta_ref[0, 0, s, :, lanes] for s in range(4)])
        values = exchange_chunks([frhs_ref[0, 0, s, :, lanes] for s in range(4)])
        for k in range(4):
            at = pl.multiple_of((4 * j + k) * 32, 32)
            g = values[k] / (9.0 * betas[k])
            BT[pl.ds(at, 32), :] = betas[k]
            G[pl.ds(at, 32), :] = g
            FA[pl.ds(at + 32, 32), :] = g * keep32
        return 0

    lax.fori_loop(0, 8, load_fine, 0)

    def pack_faces(stage):
        stage[0, 0:32, :] = FA[pl.ds(32, 32, stride=32), :]
        stage[1, 0:32, :] = FA[pl.ds(63, 32, stride=32), :]
        stage[2, 0:32, :] = FA[32:64, :]
        stage[3, 0:32, :] = FA[32 * 32 : 33 * 32, :]

    def send_faces(stage, inbox):
        return start([(*DIRS[d], stage.at[d], inbox.at[d]) for d in range(4)])

    pl.semaphore_wait(barrier, total)
    pack_faces(SB.at[0])
    wait_b = send_faces(SB.at[0], RB.at[0])

    lane8 = lane

    def pair(value, shift):
        wide = lax.broadcasted_iota(jnp.int32, value.shape, 1)
        return value + jnp.where((wide & shift) == 0, roll(value, -shift, 1), roll(value, shift, 1))

    for y in range(16):
        beta = bbeta_ref[pl.ds(y, 16, stride=16), :]
        c = beta * 0.25
        at = (y + 2) * S0 + O0
        C0[at : at + 16, :] = c
        W0[at : at + 16, :] = 1.0 / (9.0 * c)
        BR[at : at + 16, :] = brhs_ref[pl.ds(y, 16, stride=16), :]

    def restrict0(values, y):
        t = pair(values(2 + 2 * y) + values(3 + 2 * y), 1)
        T0[y * S0 : (y + 1) * S0, :] = t
        return (T0[pl.ds(y * S0 + O0, 8, stride=2), :] + T0[pl.ds(y * S0 + O0 + 1, 8, stride=2), :]) * 0.125

    def restrict1(values, y):
        t = pair(values(1 + 2 * y) + values(2 + 2 * y), 2)
        T1[y * S1 : (y + 1) * S1, :] = t
        return (T1[pl.ds(y * S1 + 4, 8, stride=2), :] + T1[pl.ds(y * S1 + 5, 8, stride=2), :]) * 0.125

    def restrict2(values, y):
        t = pair(values(2 + 2 * y) + values(3 + 2 * y), 4)
        T2[y * S2 : (y + 1) * S2, :] = t
        return (T2[pl.ds(y * S2, 4, stride=2), :] + T2[pl.ds(y * S2 + 1, 4, stride=2), :]) * 0.125

    for y in range(8):
        c = restrict0(lambda p: C0[p * S0 : (p + 1) * S0, :], y) * 0.25
        C1[(y + 5) * S1 + O1 : (y + 5) * S1 + O1 + 8, :] = c
        W1[y * 8 : y * 8 + 8, :] = 1.0 / (9.0 * c)

    def send_level1(ref, stage, inbox):
        for k in range(5):
            stage[0, k * 8 : k * 8 + 8, :] = ref[pl.ds(5 * S1 + O1 + k, 8, stride=S1), :]
            stage[1, k * 8 : k * 8 + 8, :] = ref[pl.ds(5 * S1 + O1 + 3 + k, 8, stride=S1), :]
            stage[2, k * 8 : k * 8 + 8, :] = ref[(5 + k) * S1 + O1 : (5 + k) * S1 + O1 + 8, :]
            stage[3, k * 8 : k * 8 + 8, :] = ref[(8 + k) * S1 + O1 : (8 + k) * S1 + O1 + 8, :]
        source = (0, 1, 2, 3, 2, 3, 2, 3)
        return start([(*DIRS[d], stage.at[source[d]], inbox.at[d]) for d in range(8)])

    def unpack_level1(ref, inbox):
        for k in range(5):
            part = slice(k * 8, k * 8 + 8)
            ref[pl.ds(5 * S1 + 16 + k, 8, stride=S1), :] = inbox[0, part, :]
            ref[pl.ds(5 * S1 + 3 + k, 8, stride=S1), :] = inbox[1, part, :]
            low, high = k * S1, (13 + k) * S1
            ref[high + 8 : high + 16, :] = inbox[2, part, :]
            ref[low + 8 : low + 16, :] = inbox[3, part, :]
            ref[high + 16 : high + 24, :] = inbox[4, part, :]
            ref[low + 16 : low + 24, :] = inbox[5, part, :]
            ref[high : high + 8, :] = inbox[6, part, :]
            ref[low : low + 8, :] = inbox[7, part, :]

    wait_p = send_level1(C1, SP, RP)

    def neighbours(ref, plane, rows, shift):
        c = ref[plane * rows : (plane + 1) * rows, :]
        wide = lax.broadcasted_iota(jnp.int32, (rows, 128), 1)
        total = ref[(plane + 1) * rows : (plane + 2) * rows, :] + ref[(plane - 1) * rows : plane * rows, :]
        total = total + (roll(c, 1, 0) + roll(c, -1, 0))
        low = jnp.where(wide >= shift, roll(c, shift, 1), 0.0)
        high = jnp.where(wide < 128 - shift, roll(c, -shift, 1), 0.0)
        return c, total + (low + high)

    def row_mask(rows, first, extent, count):
        at = lax.broadcasted_iota(jnp.int32, (rows, 128), 0) - first + gx * extent
        return jnp.where((at >= 0) & (at < count), 1.0, 0.0).astype(F32)

    def plane_mask(y, extent, count):
        at = y + gy * extent
        return jnp.where((at >= 0) & (at < count), 1.0, 0.0).astype(F32)

    rows0 = row_mask(S0, O0, 16, nx * 16)
    rows1 = row_mask(S1, O1, 8, nx * 8)
    rows2 = row_mask(S2, O2, 4, nx * 4)

    def post(pre, field, plane, rows, shift, mask, scale):
        c, around = neighbours(field, plane, rows, shift)
        return pre[plane * rows : (plane + 1) * rows, :] + (mask * scale) * (c * (1.0 / 3.0) + around * (1.0 / 9.0))

    def fine_around(field, y, center):
        at = pl.multiple_of(y * 32, 32)
        total = field[pl.ds(at, 32), :] + field[pl.ds(at + 64, 32), :]
        low = jnp.broadcast_to(GX[0, pl.ds(y, 1), :], (32, 128))
        high = jnp.broadcast_to(GX[1, pl.ds(y, 1), :], (32, 128))
        total = total + jnp.where(first32 > 0, low, roll(center, 1, 0)) + jnp.where(last32 > 0, high, roll(center, -1, 0))
        total = total + (pick(center, index_low) * mask_low32 + pick(center, index_high) * mask_high32)
        return total + CGZ[pl.ds(pl.multiple_of((y >> 1) * 32, 32), 32), :]

    def restrict_fine(values, y):
        at = pl.multiple_of(y * 32, 32)
        T[pl.ds(at, 32), :] = values
        t = T[pl.ds(at, 16, stride=2), :] + T[pl.ds(at + 1, 16, stride=2), :]
        return pick(t + roll(t, -1, 1), index_in) * 0.125

    def double(ref, at, value):
        ref[pl.ds(at, value.shape[0], stride=2), :] = value
        ref[pl.ds(at + 1, value.shape[0], stride=2), :] = value

    def set_ghosts(inbox):
        GX[0, :, :] = pick(inbox[1, 0:32, :], index_g[0]) * tile(mask_g[0], 4) + CB[0:32, :]
        GX[1, :, :] = pick(inbox[0, 0:32, :], index_g[1]) * tile(mask_g[1], 4) + CB[32:64, :]
        FA[0:32, :] = pick(inbox[3, 0:32, :], index_g[2]) * tile(mask_g[2], 4) + CB[64:96, :]
        FA[33 * 32 : 34 * 32, :] = pick(inbox[2, 0:32, :], index_g[3]) * tile(mask_g[3], 4) + CB[96:128, :]

    def outer(ref, d):
        if d == 0:
            return ref[pl.ds(2 * S0 + O0 - 1, 16, stride=S0), :]
        if d == 1:
            return ref[pl.ds(2 * S0 + O0 + 16, 16, stride=S0), :]
        plane = 1 if d == 2 else 18
        return ref[plane * S0 + O0 : plane * S0 + O0 + 16, :]

    def coarse_z():
        for y in range(16):
            at = (y + 2) * S0 + O0
            double(CGZ, y * 32, pick(B0[at : at + 16, :], index_cz) * tile(mask_cz, 2))

    for cycle in range(CYCLES):
        if cycle == 0:
            CGZ[...] = jnp.zeros(CGZ.shape, F32)
        else:
            pack_faces(SA)
            SA[0, 32:48, :] = B0[pl.ds(2 * S0 + O0, 16, stride=S0), :]
            SA[1, 32:48, :] = B0[pl.ds(2 * S0 + O0 + 15, 16, stride=S0), :]
            SA[2, 32:48, :] = B0[2 * S0 + O0 : 2 * S0 + O0 + 16, :]
            SA[3, 32:48, :] = B0[17 * S0 + O0 : 17 * S0 + O0 + 16, :]
            wait_a = send_faces(SA, RA)
            coarse_z()
            finish(wait_a)
            B0[pl.ds(2 * S0 + O0 + 16, 16, stride=S0), :] = RA[0, 32:48, :]
            B0[pl.ds(2 * S0 + O0 - 1, 16, stride=S0), :] = RA[1, 32:48, :]
            B0[18 * S0 + O0 : 18 * S0 + O0 + 16, :] = RA[2, 32:48, :]
            B0[1 * S0 + O0 : 1 * S0 + O0 + 16, :] = RA[3, 32:48, :]
            for d in range(4):
                double(CB, d * 32, pick(outer(B0, d), index_p) * tile(1.0 - mask_g[d], 2))
            set_ghosts(RA)

            def first_sweep(y, _):
                at = pl.multiple_of(y * 32, 32)
                center = FA[pl.ds(at + 32, 32), :]
                around = fine_around(FA, y, center)
                FB[pl.ds(at + 32, 32), :] = keep32 * (
                    G[pl.ds(at, 32), :] + center * (1.0 / 3.0) + around * (1.0 / 9.0)
                )
                return 0

            lax.fori_loop(0, 32, first_sweep, 0, unroll=2)

            def copy_back(y, _):
                at = pl.ds(pl.multiple_of(y * 32 + 32, 32), 32)
                FA[at, :] = FB[at, :]
                return 0

            lax.fori_loop(0, 32, copy_back, 0, unroll=4)
            pack_faces(SB.at[cycle])
            wait_b = send_faces(SB.at[cycle], RB.at[cycle])

        if cycle == 0:
            for y in range(16):
                at = (y + 2) * S0
                P0[at : at + S0, :] = BR[at : at + S0, :]
        else:
            for y in range(16):
                at = (y + 2) * S0
                c, around = neighbours(B0, y + 2, S0, 1)
                P0[at : at + S0, :] = BR[at : at + S0, :] - C0[at : at + S0, :] * (6.0 * c - around)

        finish(wait_b)
        set_ghosts(RB.at[cycle])

        def residual(y, _):
            def one(k):
                at = pl.multiple_of(k * 32, 32)
                center = FA[pl.ds(at + 32, 32), :]
                around = fine_around(FA, k, center)
                return BT[pl.ds(at, 32), :] * (9.0 * G[pl.ds(at, 32), :] - 6.0 * center + around)

            both = one(2 * y) + one(2 * y + 1)
            T[pl.ds(pl.multiple_of(y * 32, 32), 32), :] = both
            return 0

        lax.fori_loop(0, 16, residual, 0)
        for y in range(16):
            t = T[pl.ds(y * 32, 16, stride=2), :] + T[pl.ds(y * 32 + 1, 16, stride=2), :]
            means = pick(t + roll(t, -1, 1), index_in) * 0.125
            at = (y + 2) * S0 + O0
            P0[at : at + 16, :] = jnp.where(mask_in16 > 0, means, P0[at : at + 16, :]) * W0[at : at + 16, :]

        stage, corner = SC.at[cycle], SCC.at[cycle]
        for k in range(2):
            part = slice(k * 16, k * 16 + 16)
            stage[0, part, :] = P0[pl.ds(2 * S0 + O0 + k, 16, stride=S0), :]
            stage[1, part, :] = P0[pl.ds(2 * S0 + O0 + 14 + k, 16, stride=S0), :]
            stage[2, part, :] = P0[(2 + k) * S0 + O0 : (2 + k) * S0 + O0 + 16, :]
            stage[3, part, :] = P0[(16 + k) * S0 + O0 : (16 + k) * S0 + O0 + 16, :]
            for d in range(4):
                dx, dy = DIRS[4 + d]
                at = ((2 if dy < 0 else 16) + k) * S0 + O0 + (0 if dx < 0 else 14)
                corner[d, 2 * k : 2 * k + 2, :] = P0[at : at + 2, :]
        inbox, corners = RC.at[cycle], RCC.at[cycle]
        wait_c = start(
            [(*DIRS[d], stage.at[d], inbox.at[d]) for d in range(4)]
            + [(*DIRS[4 + d], corner.at[d], corners.at[d]) for d in range(4)]
        )
        finish(wait_c)
        for k in range(2):
            part = slice(k * 16, k * 16 + 16)
            P0[pl.ds(2 * S0 + O0 + 16 + k, 16, stride=S0), :] = inbox[0, part, :]
            P0[pl.ds(2 * S0 + O0 - 2 + k, 16, stride=S0), :] = inbox[1, part, :]
            P0[(18 + k) * S0 + O0 : (18 + k) * S0 + O0 + 16, :] = inbox[2, part, :]
            P0[k * S0 + O0 : k * S0 + O0 + 16, :] = inbox[3, part, :]
            for d in range(4):
                dx, dy = DIRS[4 + d]
                at = ((18 if dy < 0 else 0) + k) * S0 + (O0 + 16 if dx < 0 else O0 - 2)
                P0[at : at + 2, :] = corners[d, 2 * k : 2 * k + 2, :]

        def left0(plane):
            c, around = neighbours(P0, plane, S0, 1)
            return C0[plane * S0 : (plane + 1) * S0, :] * (3.0 * c + around)

        for y in range(8):
            at = (y + 5) * S1 + O1
            P1[at : at + 8, :] = restrict0(left0, y) * W1[y * 8 : y * 8 + 8, :]
        wait_d = send_level1(P1, SD.at[cycle], RD.at[cycle])
        if cycle == 0:
            finish(wait_p)
            unpack_level1(C1, RP)
            for y in range(8):
                c = restrict1(lambda p: C1[p * S1 : (p + 1) * S1, :], y) * 0.25
                C2[y * 8 : y * 8 + 8, :] = c
                W2[y * 8 : y * 8 + 8, :] = jnp.where(c > 0, 1.0 / (9.0 * jnp.where(c > 0, c, 1.0)), 0.0)
            for y in range(2):
                c = restrict2(lambda p: C2[p * S2 : (p + 1) * S2, :], y) * 0.25
                W3[y * 4 : y * 4 + 4, :] = jnp.where(c > 0, 1.0 / (9.0 * jnp.where(c > 0, c, 1.0)), 0.0)
        finish(wait_d)
        unpack_level1(P1, RD.at[cycle])

        def left1(plane):
            c, around = neighbours(P1, plane, S1, 2)
            return C1[plane * S1 : (plane + 1) * S1, :] * (3.0 * c + around)

        for y in range(8):
            P2[y * 8 : y * 8 + 8, :] = restrict1(left1, y) * W2[y * 8 : y * 8 + 8, :]

        def left2(plane):
            c, around = neighbours(P2, plane, S2, 4)
            return C2[plane * S2 : (plane + 1) * S2, :] * (3.0 * c + around)

        mine = jnp.concatenate([restrict2(left2, y) for y in range(2)], axis=0) * W3[...]
        strip = SW.at[cycle]
        strip[...] = pick(mine, (lane8 & 15) * 8)
        wait_w = start([(0, k, strip, RW.at[cycle, 3 - k]) for k in REACH])
        finish(wait_w)
        joined = jnp.where((lane8 >> 4) == 3, strip[...], 0.0)
        for k in REACH:
            joined = jnp.where((lane8 >> 4) == 3 + k, RW[cycle, 3 + k, :, :], joined)
        SX[cycle, :, :] = joined
        wait_x = start([(k, 0, SX.at[cycle], RX.at[cycle, pl.ds((3 - k) * 8, 8)]) for k in REACH])
        RX[cycle, 24:32, :] = joined
        finish(wait_x)

        first = [[RX[cycle, pl.ds(y * 4 + 1 + x, 8, stride=8), :] for x in range(2)] for y in range(2)]
        col_x = gx + row8 - 3
        col_y = gy + (lane8 >> 4) - 3
        there = (col_x >= 0) & (col_x < nx) & (row8 < 7) & (col_y >= 0) & (col_y < ny) & (lane8 < 112)
        mask3 = jnp.where(there, 1.0, 0.0).astype(F32)
        e = first
        for sweep in range(SWEEPS - 1):
            new = [[None, None], [None, None]]
            for y in range(2):
                for x in range(2):
                    c, ex, ey = e[y][x], e[y][1 - x], e[1 - y][x]
                    around = ex + roll(ex, 1 if x == 0 else -1, 0) + ey + roll(ey, 16 if y == 0 else -16, 1)
                    around = around + jnp.where((lane8 & 15) > 0, roll(c, 1, 1), 0.0)
                    around = around + jnp.where((lane8 & 15) < 15, roll(c, -1, 1), 0.0)
                    new[y][x] = first[y][x] + mask3 * (c * (1.0 / 3.0) + around * (1.0 / 9.0))
            e = new

        from_one = jnp.where(row8 < 2, 2, 3)
        from_zero = jnp.where(row8 < 4, 3, 4)
        for k, (column, y) in enumerate(((2, 1), (3, 0), (3, 1), (4, 0))):
            lanes = column * 16 + (lane8 >> 3)
            zero, one = pick(e[y][0], lanes), pick(e[y][1], lanes)
            zero = jnp.take_along_axis(zero, from_zero, axis=0, mode="promise_in_bounds")
            one = jnp.take_along_axis(one, from_one, axis=0, mode="promise_in_bounds")
            up = jnp.where((row8 & 2) == 0, one, zero)
            for plane in (2 * k, 2 * k + 1):
                E2[plane * 8 : plane * 8 + 8, :] = P2[plane * 8 : plane * 8 + 8, :] + up
        for plane in range(1, 7):
            up = post(P2, E2, plane, S2, 4, rows2, plane_mask(plane - 2, 4, ny * 4))
            at = plane * S1
            double(U1, at + 4, up)
            for fine in (2 * plane + 1, 2 * plane + 2):
                E1[fine * S1 : (fine + 1) * S1, :] = P1[fine * S1 : (fine + 1) * S1, :] + U1[at : at + S1, :]
        for plane in range(4, 14):
            at = plane * S1
            U1[at : at + S1, :] = post(P1, E1, plane, S1, 2, rows1, plane_mask(plane - 5, 8, ny * 8))
            value = U1[at + 7 : at + 17, :]
            fine = 2 * (plane - 4)
            double(E0, fine * S0 + 2, value)
            up = E0[fine * S0 : (fine + 1) * S0, :]
            E0[(fine + 1) * S0 : (fine + 2) * S0, :] = up + P0[(fine + 1) * S0 : (fine + 2) * S0, :]
            E0[fine * S0 : (fine + 1) * S0, :] = up + P0[fine * S0 : (fine + 1) * S0, :]
        for plane in range(1, 19):
            at = plane * S0
            P0[at : at + S0, :] = post(P0, E0, plane, S0, 1, rows0, plane_mask(plane - 2, 16, ny * 16))
            B0[at : at + S0, :] = B0[at : at + S0, :] + P0[at : at + S0, :]

        for y in range(16):
            at = (y + 2) * S0 + O0
            double(PC, y * 32, pick(P0[at : at + 16, :], index_p))
        coarse_z()
        for d in range(4):
            double(T, d * 32, pick(outer(P0, d), index_p))
        GX[0, :, :] = GX[0, :, :] + T[0:32, :]
        GX[1, :, :] = GX[1, :, :] + T[32:64, :]
        FB[0:32, :] = FA[0:32, :] + T[64:96, :]
        FB[33 * 32 : 34 * 32, :] = FA[33 * 32 : 34 * 32, :] + T[96:128, :]

        def correct(y, _):
            at = pl.ds(pl.multiple_of(y * 32 + 32, 32), 32)
            FB[at, :] = keep32 * (FA[at, :] + PC[pl.ds(pl.multiple_of((y >> 1) * 32, 32), 32), :])
            return 0

        lax.fori_loop(0, 32, correct, 0, unroll=4)

        def last_sweep(y, _):
            def one(k):
                at = pl.multiple_of(k * 32, 32)
                center = FB[pl.ds(at + 32, 32), :]
                around = fine_around(FB, k, center)
                new = keep32 * (G[pl.ds(at, 32), :] + center * (1.0 / 3.0) + around * (1.0 / 9.0))
                FA[pl.ds(at + 32, 32), :] = new
                return new

            both = one(2 * y) + one(2 * y + 1)
            T[pl.ds(pl.multiple_of(y * 32, 32), 32), :] = both
            return 0

        lax.fori_loop(0, 16, last_sweep, 0)
        for y in range(16):
            t = T[pl.ds(y * 32, 16, stride=2), :] + T[pl.ds(y * 32 + 1, 16, stride=2), :]
            means = pick(t + roll(t, -1, 1), index_in) * 0.125
            at = (y + 2) * S0 + O0
            B0[at : at + 16, :] = jnp.where(mask_in16 > 0, means, B0[at : at + 16, :])

    def store_fine(j, _):
        planes = exchange_chunks([FA[pl.ds(pl.multiple_of((4 * j + k + 1) * 32, 32), 32), :] for k in range(4)])
        for s in range(4):
            fout_ref[0, 0, s, :, pl.ds(pl.multiple_of(j * 128, 128), 128)] = planes[s]
        return 0

    lax.fori_loop(0, 8, store_fine, 0)
    for y in range(16):
        at = (y + 2) * S0 + O0
        bout_ref[pl.ds(y, 16, stride=16), :] = B0[at : at + 16, :]
    for dx, dy, copy in pending:
        pl.when(inside(dx, dy))(lambda copy=copy: copy().wait_send())


def solution(mesh):
    nx, ny = mesh.shape["gx"], mesh.shape["gy"]

    def local(fine_rhs, fine_beta, base_rhs, base_beta, slot_site, ghost_list, box_count):
        vmem = pl.BlockSpec(memory_space=pltpu.VMEM)
        smem = pl.BlockSpec(memory_space=pltpu.SMEM)

        def rows(*shape):
            return pltpu.VMEM((*shape, 128), F32)

        fine, base = pl.pallas_call(
            lambda *refs: kernel(nx, ny, *refs),
            out_shape=(
                jax.ShapeDtypeStruct(fine_rhs.shape, F32),
                jax.ShapeDtypeStruct((256, 128), F32),
            ),
            in_specs=[smem] * 3 + [vmem] * 4,
            out_specs=(vmem, vmem),
            scratch_shapes=[
                rows(34 * 32),
                rows(34 * 32),
                rows(32 * 32),
                rows(32 * 32),
                rows(16 * 32),
                rows(16 * 32),
                rows(16 * 32),
                rows(2, 32),
                rows(4 * 32),
                rows(20 * S0),
                rows(20 * S0),
                rows(20 * S0),
                rows(20 * S0),
                rows(20 * S0),
                rows(20 * S0),
                rows(8 * S0),
                rows(18 * S1),
                rows(64),
                rows(18 * S1),
                rows(18 * S1),
                rows(18 * S1),
                rows(8 * S1),
                rows(64),
                rows(64),
                rows(64),
                rows(64),
                rows(16),
                rows(8),
                rows(4, 40),
                rows(8, 40),
                rows(4, 48),
                rows(4, 48),
                rows(2, 4, 32),
                rows(2, 4, 32),
                rows(2, 4, 32),
                rows(2, 4, 8),
                rows(2, 4, 32),
                rows(2, 4, 8),
                rows(2, 4, 40),
                rows(2, 8, 40),
                rows(2, 8),
                rows(2, 7, 8),
                rows(2, 8),
                rows(2, 64),
                pltpu.SemaphoreType.DMA((SEM_COUNT,)),
                pltpu.SemaphoreType.DMA((SEM_COUNT,)),
            ],
            compiler_params=pltpu.CompilerParams(
                collective_id=0, has_side_effects=True, vmem_limit_bytes=48 * 1024 * 1024
            ),
            name="vcycles",
        )(
            slot_site,
            ghost_list,
            box_count,
            fine_rhs,
            fine_beta,
            base_rhs.reshape(256, 128),
            base_beta.reshape(256, 128),
        )
        return fine, base.reshape(16, 16, 128)

    return jax.shard_map(
        local,
        mesh=mesh,
        in_specs=(
            P("gx", "gy", None, None, None),
            P("gx", "gy", None, None, None),
            P("gx", "gy", None),
            P("gx", "gy", None),
            P("gx", "gy", None),
            P("gx", "gy", None, None),
            P("gx", "gy"),
        ),
        out_specs=(P("gx", "gy", None, None, None), P("gx", "gy", None)),
        check_vma=False,
    )
```

time: 935 us -> 72.7 us (0.08)
  the two profiles are of different devices: /device:TPU:56 before, /device:TPU:1 now
where the time goes in v1:
time: 72.7 us; the launch traced here: 72.4 us
  Pallas kernels  65.1 us (90%)
  local copies, waits for them, and re-layouts  6.01 us (8%)
  between operations  1.31 us (2%)
    pallas_call x1, Pallas kernels, local(): pl.pallas_call(lambda *refs: kernel(nx, ny, *refs), out_shape=(jax.ShapeD...  65.1 us
    unnamed x14, local copies, waits for them, and re-layouts  6.01 us

profile of v1, /device:TPU:1, one launch (start us, length us, event | category | flops | bytes accessed | tf_op | source)
XLA Modules:
  0.0 72.4 jit_solution(4105377867821801203)
XLA Ops:
  1.3 0.0 copy-start.4
  1.3 0.0 copy-start.5
  1.3 0.7 copy-done.4
  2.0 0.0 copy-done.5
  2.0 0.0 copy-start
  2.0 1.0 %copy-done = f32[1,1,4,32,1024]{4,3,2,1,0:T(8,128)S(1)} copy-done((f32[1,1,4,32,1024]{4,3,2,1,0:T(8,128)S(1)}, f32[1,1,4,32,1024]{4,3,2,1,0:T(8,128)}, u32[]{:S(2)}) %copy-start) | copy-done | bytes 524312
  3.0 0.0 copy-start.1
  3.0 1.0 %copy-done.1 = f32[1,1,4,32,1024]{4,3,2,1,0:T(8,128)S(1)} copy-done((f32[1,1,4,32,1024]{4,3,2,1,0:T(8,128)S(1)}, f32[1,1,4,32,1024]{4,3,2,1,0:T(8,128)}, u32[]{:S(2)}) %copy-start.1) | copy-done | bytes 524312
  4.0 0.0 copy-start.2
  4.1 0.9 %copy-done.2 = f32[16,16,128]{2,1,0:T(8,128)S(1)} copy-done((f32[16,16,128]{2,1,0:T(8,128)S(1)}, f32[16,16,128]{2,1,0:T(8,128)}, u32[]{:S(2)}) %copy-start.2) | copy-done | bytes 131096
  5.0 0.0 copy-start.3
  5.0 0.9 %copy-done.3 = f32[16,16,128]{2,1,0:T(8,128)S(1)} copy-done((f32[16,16,128]{2,1,0:T(8,128)S(1)}, f32[16,16,128]{2,1,0:T(8,128)}, u32[]{:S(2)}) %copy-start.3) | copy-done | bytes 131096
  5.9 65.1 %vcycles.1 = (f32[1,1,4,32,1024]{4,3,2,1,0:T(8,128)S(1)}, f32[256,128]{1,0:T(8,128)S(1)}) custom-call(s32[1,1,4]{2,1,0:T(1,128)S(1)} %copy-done.5, s32[1,1,4,6]{3,2,1,0:T(4,128)S(1)} %copy-done.4, s32[1,1]{1,0:T(1,128)S(6)} %copy.11.refs_2_, f32[1,1,4,32,1024]{4,3,2,1,0:T(8,128)S(1)} %copy-done, f32[1,1,4,32,1024]{4,3,2,1,0:T(8,128)S(1)} %copy-done.1, ...), custom_call_target="tpu_custom_call" | custom-call | tf_op jit(solution)/shard_map/vcycles/pallas_call | solution.py:616
  71.0 0.8 %copy.12 = f32[1,1,4,32,1024]{4,3,2,1,0:T(8,128)} copy(f32[1,1,4,32,1024]{4,3,2,1,0:T(8,128)S(1)} %get-tuple-element.8) | data formatting | bytes 1048576
  71.8 0.7 copy.13
Async XLA Ops:
  1.3 0.7 copy-start.4
  1.3 0.7 copy-start.5
  2.0 1.0 %copy-start = (f32[1,1,4,32,1024]{4,3,2,1,0:T(8,128)S(1)}, f32[1,1,4,32,1024]{4,3,2,1,0:T(8,128)}, u32[]{:S(2)}) copy-start(f32[1,1,4,32,1024]{4,3,2,1,0:T(8,128)} %refs_3_.1) | copy-start | bytes 1572868
  3.0 1.0 %copy-start.1 = (f32[1,1,4,32,1024]{4,3,2,1,0:T(8,128)S(1)}, f32[1,1,4,32,1024]{4,3,2,1,0:T(8,128)}, u32[]{:S(2)}) copy-start(f32[1,1,4,32,1024]{4,3,2,1,0:T(8,128)} %refs_4_.1) | copy-start | bytes 1572868
  4.0 0.9 %copy-start.2 = (f32[16,16,128]{2,1,0:T(8,128)S(1)}, f32[16,16,128]{2,1,0:T(8,128)}, u32[]{:S(2)}) copy-start(f32[16,16,128]{2,1,0:T(8,128)} %param.9) | copy-start | bytes 393220
  5.0 0.9 %copy-start.3 = (f32[16,16,128]{2,1,0:T(8,128)S(1)}, f32[16,16,128]{2,1,0:T(8,128)}, u32[]{:S(2)}) copy-start(f32[16,16,128]{2,1,0:T(8,128)} %param.10) | copy-start | bytes 393220

commit v2 on v1

--- a/solution.py
+++ b/solution.py
@@ -43,12 +43,17 @@
     site_ref,
     link_ref,
     count_ref,
+    frhs_hbm,
+    fbeta_hbm,
+    brhs_hbm,
+    bbeta_hbm,
+    fout_ref,
+    bout_ref,
     frhs_ref,
     fbeta_ref,
     brhs_ref,
     bbeta_ref,
-    fout_ref,
-    bout_ref,
+    fetch_sem,
     FA,
     FB,
     G,
@@ -141,9 +146,16 @@
         for dx, dy, copy in sent:
             pl.when(inside(-dx, -dy))(lambda copy=copy: copy().wait_recv())
 
-    for ref in (B0, BR, C0, W0, P0, E0, C1, P1, E1, U1, FA, FB, GX, CB, SCC, RX):
-        ref[...] = jnp.zeros(ref.shape, F32)
-    for ref in (RP, RA, RB, RC, RCC, RD, RW):
+    fetches = [
+        pltpu.make_async_copy(fbeta_hbm.at[0, 0], fbeta_ref, fetch_sem.at[0]),
+        pltpu.make_async_copy(frhs_hbm.at[0, 0], frhs_ref, fetch_sem.at[1]),
+        pltpu.make_async_copy(bbeta_hbm, bbeta_ref, fetch_sem.at[2]),
+        pltpu.make_async_copy(brhs_hbm, brhs_ref, fetch_sem.at[3]),
+    ]
+    for fetch in fetches:
+        fetch.start()
+
+    for ref in (RP, RA, RB, RC, RCC, RD, RW, RX):
         ref[...] = jnp.zeros(ref.shape, F32)
 
     barrier = pltpu.get_barrier_semaphore()
@@ -156,6 +168,9 @@
 
         pl.when(there)(greet)
         total = total + there.astype(jnp.int32)
+
+    for ref in (B0, BR, C0, W0, P0, E0, C1, P1, E1, U1, FA, FB, GX, CB, SCC):
+        ref[...] = jnp.zeros(ref.shape, F32)
 
     lane = lax.broadcasted_iota(jnp.int32, (8, 128), 1)
     row8 = lax.broadcasted_iota(jnp.int32, (8, 128), 0)
@@ -214,8 +229,8 @@
 
     def load_fine(j, _):
         lanes = pl.ds(pl.multiple_of(j * 128, 128), 128)
-        betas = exchange_chunks([fbeta_ref[0, 0, s, :, lanes] for s in range(4)])
-        values = exchange_chunks([frhs_ref[0, 0, s, :, lanes] for s in range(4)])
+        betas = exchange_chunks([fbeta_ref[s, :, lanes] for s in range(4)])
+        values = exchange_chunks([frhs_ref[s, :, lanes] for s in range(4)])
         for k in range(4):
             at = pl.multiple_of((4 * j + k) * 32, 32)
             g = values[k] / (9.0 * betas[k])
@@ -224,6 +239,8 @@
             FA[pl.ds(at + 32, 32), :] = g * keep32
         return 0
 
+    fetches[0].wait()
+    fetches[1].wait()
     lax.fori_loop(0, 8, load_fine, 0)
 
     def pack_faces(stage):
@@ -245,6 +262,8 @@
         wide = lax.broadcasted_iota(jnp.int32, value.shape, 1)
         return value + jnp.where((wide & shift) == 0, roll(value, -shift, 1), roll(value, shift, 1))
 
+    fetches[2].wait()
+    fetches[3].wait()
     for y in range(16):
         beta = bbeta_ref[pl.ds(y, 16, stride=16), :]
         c = beta * 0.25
@@ -322,11 +341,11 @@
         c, around = neighbours(field, plane, rows, shift)
         return pre[plane * rows : (plane + 1) * rows, :] + (mask * scale) * (c * (1.0 / 3.0) + around * (1.0 / 9.0))
 
-    def fine_around(field, y, center):
+    def fine_around(field, y, center, edges=True):
         at = pl.multiple_of(y * 32, 32)
         total = field[pl.ds(at, 32), :] + field[pl.ds(at + 64, 32), :]
-        low = jnp.broadcast_to(GX[0, pl.ds(y, 1), :], (32, 128))
-        high = jnp.broadcast_to(GX[1, pl.ds(y, 1), :], (32, 128))
+        low = jnp.broadcast_to(GX[0, pl.ds(y, 1), :], (32, 128)) if edges else 0.0
+        high = jnp.broadcast_to(GX[1, pl.ds(y, 1), :], (32, 128)) if edges else 0.0
         total = total + jnp.where(first32 > 0, low, roll(center, 1, 0)) + jnp.where(last32 > 0, high, roll(center, -1, 0))
         total = total + (pick(center, index_low) * mask_low32 + pick(center, index_high) * mask_high32)
         return total + CGZ[pl.ds(pl.multiple_of((y >> 1) * 32, 32), 32), :]
@@ -346,6 +365,10 @@
         GX[1, :, :] = pick(inbox[0, 0:32, :], index_g[1]) * tile(mask_g[1], 4) + CB[32:64, :]
         FA[0:32, :] = pick(inbox[3, 0:32, :], index_g[2]) * tile(mask_g[2], 4) + CB[64:96, :]
         FA[33 * 32 : 34 * 32, :] = pick(inbox[2, 0:32, :], index_g[3]) * tile(mask_g[3], 4) + CB[96:128, :]
+
+    def clear_y_ghosts():
+        FA[0:32, :] = jnp.zeros((32, 128), F32)
+        FA[33 * 32 : 34 * 32, :] = jnp.zeros((32, 128), F32)
 
     def outer(ref, d):
         if d == 0:
@@ -371,6 +394,18 @@
             SA[3, 32:48, :] = B0[17 * S0 + O0 : 17 * S0 + O0 + 16, :]
             wait_a = send_faces(SA, RA)
             coarse_z()
+            clear_y_ghosts()
+
+            def first_sweep(y, _):
+                at = pl.multiple_of(y * 32, 32)
+                center = FA[pl.ds(at + 32, 32), :]
+                around = fine_around(FA, y, center, False)
+                FB[pl.ds(at + 32, 32), :] = keep32 * (
+                    G[pl.ds(at, 32), :] + center * (1.0 / 3.0) + around * (1.0 / 9.0)
+                )
+                return 0
+
+            lax.fori_loop(0, 32, first_sweep, 0, unroll=2)
             finish(wait_a)
             B0[pl.ds(2 * S0 + O0 + 16, 16, stride=S0), :] = RA[0, 32:48, :]
             B0[pl.ds(2 * S0 + O0 - 1, 16, stride=S0), :] = RA[1, 32:48, :]
@@ -380,23 +415,13 @@
                 double(CB, d * 32, pick(outer(B0, d), index_p) * tile(1.0 - mask_g[d], 2))
             set_ghosts(RA)
 
-            def first_sweep(y, _):
-                at = pl.multiple_of(y * 32, 32)
-                center = FA[pl.ds(at + 32, 32), :]
-                around = fine_around(FA, y, center)
-                FB[pl.ds(at + 32, 32), :] = keep32 * (
-                    G[pl.ds(at, 32), :] + center * (1.0 / 3.0) + around * (1.0 / 9.0)
-                )
-                return 0
-
-            lax.fori_loop(0, 32, first_sweep, 0, unroll=2)
-
-            def copy_back(y, _):
-                at = pl.ds(pl.multiple_of(y * 32 + 32, 32), 32)
-                FA[at, :] = FB[at, :]
-                return 0
-
-            lax.fori_loop(0, 32, copy_back, 0, unroll=4)
+            ninth = keep32 * (1.0 / 9.0)
+            FB[32:64, :] = FB[32:64, :] + ninth * FA[0:32, :]
+            FB[32 * 32 : 33 * 32, :] = FB[32 * 32 : 33 * 32, :] + ninth * FA[33 * 32 : 34 * 32, :]
+            for d, first in enumerate((32, 63)):
+                face = pl.ds(first, 32, stride=32)
+                FB[face, :] = FB[face, :] + ninth * GX[d, :, :]
+            FA, FB = FB, FA
             pack_faces(SB.at[cycle])
             wait_b = send_faces(SB.at[cycle], RB.at[cycle])
 
@@ -410,14 +435,13 @@
                 c, around = neighbours(B0, y + 2, S0, 1)
                 P0[at : at + S0, :] = BR[at : at + S0, :] - C0[at : at + S0, :] * (6.0 * c - around)
 
-        finish(wait_b)
-        set_ghosts(RB.at[cycle])
+        clear_y_ghosts()
 
         def residual(y, _):
             def one(k):
                 at = pl.multiple_of(k * 32, 32)
                 center = FA[pl.ds(at + 32, 32), :]
-                around = fine_around(FA, k, center)
+                around = fine_around(FA, k, center, False)
                 return BT[pl.ds(at, 32), :] * (9.0 * G[pl.ds(at, 32), :] - 6.0 * center + around)
 
             both = one(2 * y) + one(2 * y + 1)
@@ -425,6 +449,17 @@
             return 0
 
         lax.fori_loop(0, 16, residual, 0)
+        finish(wait_b)
+        set_ghosts(RB.at[cycle])
+        T[0:32, :] = T[0:32, :] + BT[0:32, :] * FA[0:32, :]
+        T[480:512, :] = T[480:512, :] + BT[31 * 32 : 32 * 32, :] * FA[33 * 32 : 34 * 32, :]
+        for d, first in enumerate((0, 31)):
+            face = pl.ds(first, 16, stride=32)
+            T[face, :] = (
+                T[face, :]
+                + BT[pl.ds(first, 16, stride=64), :] * GX[d, pl.ds(0, 16, stride=2), :]
+                + BT[pl.ds(first + 32, 16, stride=64), :] * GX[d, pl.ds(1, 16, stride=2), :]
+            )
         for y in range(16):
             t = T[pl.ds(y * 32, 16, stride=2), :] + T[pl.ds(y * 32 + 1, 16, stride=2), :]
             means = pick(t + roll(t, -1, 1), index_in) * 0.125
@@ -443,10 +478,8 @@
                 at = ((2 if dy < 0 else 16) + k) * S0 + O0 + (0 if dx < 0 else 14)
                 corner[d, 2 * k : 2 * k + 2, :] = P0[at : at + 2, :]
         inbox, corners = RC.at[cycle], RCC.at[cycle]
-        wait_c = start(
-            [(*DIRS[d], stage.at[d], inbox.at[d]) for d in range(4)]
-            + [(*DIRS[4 + d], corner.at[d], corners.at[d]) for d in range(4)]
-        )
+        wait_c = start([(*DIRS[d], stage.at[d], inbox.at[d]) for d in range(4)])
+        wait_cc = start([(*DIRS[4 + d], corner.at[d], corners.at[d]) for d in range(4)])
         finish(wait_c)
         for k in range(2):
             part = slice(k * 16, k * 16 + 16)
@@ -454,10 +487,6 @@
             P0[pl.ds(2 * S0 + O0 - 2 + k, 16, stride=S0), :] = inbox[1, part, :]
             P0[(18 + k) * S0 + O0 : (18 + k) * S0 + O0 + 16, :] = inbox[2, part, :]
             P0[k * S0 + O0 : k * S0 + O0 + 16, :] = inbox[3, part, :]
-            for d in range(4):
-                dx, dy = DIRS[4 + d]
-                at = ((18 if dy < 0 else 0) + k) * S0 + (O0 + 16 if dx < 0 else O0 - 2)
-                P0[at : at + 2, :] = corners[d, 2 * k : 2 * k + 2, :]
 
         def left0(plane):
             c, around = neighbours(P0, plane, S0, 1)
@@ -477,6 +506,12 @@
             for y in range(2):
                 c = restrict2(lambda p: C2[p * S2 : (p + 1) * S2, :], y) * 0.25
                 W3[y * 4 : y * 4 + 4, :] = jnp.where(c > 0, 1.0 / (9.0 * jnp.where(c > 0, c, 1.0)), 0.0)
+        finish(wait_cc)
+        for k in range(2):
+            for d in range(4):
+                dx, dy = DIRS[4 + d]
+                at = ((18 if dy < 0 else 0) + k) * S0 + (O0 + 16 if dx < 0 else O0 - 2)
+                P0[at : at + 2, :] = corners[d, 2 * k : 2 * k + 2, :]
         finish(wait_d)
         unpack_level1(P1, RD.at[cycle])
 
@@ -619,9 +654,14 @@
                 jax.ShapeDtypeStruct(fine_rhs.shape, F32),
                 jax.ShapeDtypeStruct((256, 128), F32),
             ),
-            in_specs=[smem] * 3 + [vmem] * 4,
+            in_specs=[smem] * 3 + [pl.BlockSpec(memory_space=pltpu.HBM)] * 4,
             out_specs=(vmem, vmem),
             scratch_shapes=[
+                pltpu.VMEM(fine_rhs.shape[2:], F32),
+                pltpu.VMEM(fine_rhs.shape[2:], F32),
+                rows(256),
+                rows(256),
+                pltpu.SemaphoreType.DMA((4,)),
                 rows(34 * 32),
                 rows(34 * 32),
                 rows(32 * 32),
@@ -670,17 +710,17 @@
                 pltpu.SemaphoreType.DMA((SEM_COUNT,)),
             ],
             compiler_params=pltpu.CompilerParams(
-                collective_id=0, has_side_effects=True, vmem_limit_bytes=48 * 1024 * 1024
+                collective_id=0, has_side_effects=True, vmem_limit_bytes=48_000_000
             ),
             name="vcycles",
         )(
-            slot_site,
-            ghost_list,
+            pltpu.with_memory_space_constraint(slot_site, pltpu.HBM),
+            pltpu.with_memory_space_constraint(ghost_list, pltpu.HBM),
             box_count,
-            fine_rhs,
-            fine_beta,
-            base_rhs.reshape(256, 128),
-            base_beta.reshape(256, 128),
+            pltpu.with_memory_space_constraint(fine_rhs, pltpu.HBM),
+            pltpu.with_memory_space_constraint(fine_beta, pltpu.HBM),
+            pltpu.with_memory_space_constraint(base_rhs.reshape(256, 128), pltpu.HBM),
+            pltpu.with_memory_space_constraint(base_beta.reshape(256, 128), pltpu.HBM),
         )
         return fine, base.reshape(16, 16, 128)
 

time: 72.7 us -> 61.4 us (0.84)
  Pallas kernels: 65.1 us -> 58.5 us
  local copies, waits for them, and re-layouts: 6.01 us -> 1.45 us
    pallas_call x1, Pallas kernels: 65.1 us -> 58.5 us  [local(): pl.pallas_call(lambda *refs: kernel(nx, ny, *refs), out_shape=(jax.ShapeD...]
    unnamed x14 -> x2, local copies, waits for them, and re-layouts: 6.01 us -> 1.45 us
where the time goes in v2:
time: 61.4 us; the launch traced here: 61.3 us
  Pallas kernels  58.5 us (95%)
  local copies, waits for them, and re-layouts  1.45 us (2%)
  between operations  1.29 us (2%)
    pallas_call x1, Pallas kernels, local(): pl.pallas_call(lambda *refs: kernel(nx, ny, *refs), out_shape=(jax.ShapeD...  58.5 us
    unnamed x2, local copies, waits for them, and re-layouts  1.45 us

profile of v2, /device:TPU:1, one launch (start us, length us, event | category | flops | bytes accessed | tf_op | source)
XLA Modules:
  0.0 61.3 jit_solution(2447158359199734666)
XLA Ops:
  1.3 58.5 %vcycles.1 = (f32[1,1,4,32,1024]{4,3,2,1,0:T(8,128)S(1)}, f32[256,128]{1,0:T(8,128)S(1)}) custom-call(s32[1,1,4]{2,1,0:T(1,128)} %refs_0_.1, s32[1,1,4,6]{3,2,1,0:T(4,128)} %refs_1_.1, s32[1,1]{1,0:T(1,128)S(6)} %copy.11.refs_2_, f32[1,1,4,32,1024]{4,3,2,1,0:T(8,128)} %refs_3_.1, f32[1,1,4,32,1024]{4,3,2,1,0:T(8,128)} %refs_4_.1, f32[256,128]{1,0:T(8,128)} %bitcast.4, ...), custom_call_target="tpu_custom_call" | custom-call | tf_op jit(solution)/shard_map/vcycles/pallas_call | solution.py:651
  59.8 0.8 %copy.12 = f32[1,1,4,32,1024]{4,3,2,1,0:T(8,128)} copy(f32[1,1,4,32,1024]{4,3,2,1,0:T(8,128)S(1)} %get-tuple-element.8) | data formatting | bytes 1048576
  60.6 0.7 %copy.13 = f32[16,16,128]{2,1,0:T(8,128)} copy(f32[16,16,128]{2,1,0:T(8,128)S(1)} %bitcast.3) | data formatting | bytes 262144

commit v3 on v2

--- a/solution.py
+++ b/solution.py
@@ -241,7 +241,7 @@
 
     fetches[0].wait()
     fetches[1].wait()
-    lax.fori_loop(0, 8, load_fine, 0)
+    lax.fori_loop(0, 8, load_fine, 0, unroll=2)
 
     def pack_faces(stage):
         stage[0, 0:32, :] = FA[pl.ds(32, 32, stride=32), :]
@@ -292,27 +292,41 @@
         C1[(y + 5) * S1 + O1 : (y + 5) * S1 + O1 + 8, :] = c
         W1[y * 8 : y * 8 + 8, :] = 1.0 / (9.0 * c)
 
+    odd = (lane & 1) == 1
+
     def send_level1(ref, stage, inbox):
-        for k in range(5):
-            stage[0, k * 8 : k * 8 + 8, :] = ref[pl.ds(5 * S1 + O1 + k, 8, stride=S1), :]
-            stage[1, k * 8 : k * 8 + 8, :] = ref[pl.ds(5 * S1 + O1 + 3 + k, 8, stride=S1), :]
-            stage[2, k * 8 : k * 8 + 8, :] = ref[(5 + k) * S1 + O1 : (5 + k) * S1 + O1 + 8, :]
-            stage[3, k * 8 : k * 8 + 8, :] = ref[(8 + k) * S1 + O1 : (8 + k) * S1 + O1 + 8, :]
+        def fill(d, tiles):
+            stage[d, 0:8, :] = jnp.where(odd, tiles[1], tiles[0])
+            stage[d, 8:16, :] = jnp.where(odd, tiles[3], tiles[2])
+            stage[d, 16:24, :] = tiles[4]
+
+        fill(0, [ref[pl.ds(5 * S1 + O1 + k, 8, stride=S1), :] for k in range(5)])
+        fill(1, [ref[pl.ds(5 * S1 + O1 + 3 + k, 8, stride=S1), :] for k in range(5)])
+        fill(2, [ref[(5 + k) * S1 + O1 : (5 + k) * S1 + O1 + 8, :] for k in range(5)])
+        fill(3, [ref[(8 + k) * S1 + O1 : (8 + k) * S1 + O1 + 8, :] for k in range(5)])
         source = (0, 1, 2, 3, 2, 3, 2, 3)
         return start([(*DIRS[d], stage.at[source[d]], inbox.at[d]) for d in range(8)])
 
     def unpack_level1(ref, inbox):
+        def tiles(d):
+            out = []
+            for k in range(2):
+                both = inbox[d, k * 8 : k * 8 + 8, :]
+                out.append(jnp.where(odd, roll(both, 1, 1), both))
+                out.append(jnp.where(odd, both, roll(both, -1, 1)))
+            return out + [inbox[d, 16:24, :]]
+
+        got = [tiles(d) for d in range(8)]
         for k in range(5):
-            part = slice(k * 8, k * 8 + 8)
-            ref[pl.ds(5 * S1 + 16 + k, 8, stride=S1), :] = inbox[0, part, :]
-            ref[pl.ds(5 * S1 + 3 + k, 8, stride=S1), :] = inbox[1, part, :]
+            ref[pl.ds(5 * S1 + 16 + k, 8, stride=S1), :] = got[0][k]
+            ref[pl.ds(5 * S1 + 3 + k, 8, stride=S1), :] = got[1][k]
             low, high = k * S1, (13 + k) * S1
-            ref[high + 8 : high + 16, :] = inbox[2, part, :]
-            ref[low + 8 : low + 16, :] = inbox[3, part, :]
-            ref[high + 16 : high + 24, :] = inbox[4, part, :]
-            ref[low + 16 : low + 24, :] = inbox[5, part, :]
-            ref[high : high + 8, :] = inbox[6, part, :]
-            ref[low : low + 8, :] = inbox[7, part, :]
+            ref[high + 8 : high + 16, :] = got[2][k]
+            ref[low + 8 : low + 16, :] = got[3][k]
+            ref[high + 16 : high + 24, :] = got[4][k]
+            ref[low + 16 : low + 24, :] = got[5][k]
+            ref[high : high + 8, :] = got[6][k]
+            ref[low : low + 8, :] = got[7][k]
 
     wait_p = send_level1(C1, SP, RP)
 
@@ -378,10 +392,10 @@
         plane = 1 if d == 2 else 18
         return ref[plane * S0 + O0 : plane * S0 + O0 + 16, :]
 
-    def coarse_z():
+    def coarse_z(ref):
         for y in range(16):
             at = (y + 2) * S0 + O0
-            double(CGZ, y * 32, pick(B0[at : at + 16, :], index_cz) * tile(mask_cz, 2))
+            double(CGZ, y * 32, pick(ref[at : at + 16, :], index_cz) * tile(mask_cz, 2))
 
     for cycle in range(CYCLES):
         if cycle == 0:
@@ -393,7 +407,7 @@
             SA[2, 32:48, :] = B0[2 * S0 + O0 : 2 * S0 + O0 + 16, :]
             SA[3, 32:48, :] = B0[17 * S0 + O0 : 17 * S0 + O0 + 16, :]
             wait_a = send_faces(SA, RA)
-            coarse_z()
+            coarse_z(B0)
             clear_y_ghosts()
 
             def first_sweep(y, _):
@@ -405,7 +419,7 @@
                 )
                 return 0
 
-            lax.fori_loop(0, 32, first_sweep, 0, unroll=2)
+            lax.fori_loop(0, 32, first_sweep, 0, unroll=4)
             finish(wait_a)
             B0[pl.ds(2 * S0 + O0 + 16, 16, stride=S0), :] = RA[0, 32:48, :]
             B0[pl.ds(2 * S0 + O0 - 1, 16, stride=S0), :] = RA[1, 32:48, :]
@@ -448,7 +462,7 @@
             T[pl.ds(pl.multiple_of(y * 32, 32), 32), :] = both
             return 0
 
-        lax.fori_loop(0, 16, residual, 0)
+        lax.fori_loop(0, 16, residual, 0, unroll=2)
         finish(wait_b)
         set_ghosts(RB.at[cycle])
         T[0:32, :] = T[0:32, :] + BT[0:32, :] * FA[0:32, :]
@@ -480,6 +494,17 @@
         inbox, corners = RC.at[cycle], RCC.at[cycle]
         wait_c = start([(*DIRS[d], stage.at[d], inbox.at[d]) for d in range(4)])
         wait_cc = start([(*DIRS[4 + d], corner.at[d], corners.at[d]) for d in range(4)])
+
+        def before(y, _):
+            at = pl.multiple_of(y * 32, 32)
+            center = FA[pl.ds(at + 32, 32), :]
+            around = fine_around(FA, y, center)
+            FB[pl.ds(at + 32, 32), :] = keep32 * (
+                G[pl.ds(at, 32), :] + center * (1.0 / 3.0) + around * (1.0 / 9.0)
+            )
+            return 0
+
+        lax.fori_loop(0, 32, before, 0, unroll=4)
         finish(wait_c)
         for k in range(2):
             part = slice(k * 16, k * 16 + 16)
@@ -588,36 +613,33 @@
 
         for y in range(16):
             at = (y + 2) * S0 + O0
-            double(PC, y * 32, pick(P0[at : at + 16, :], index_p))
-        coarse_z()
-        for d in range(4):
-            double(T, d * 32, pick(outer(P0, d), index_p))
-        GX[0, :, :] = GX[0, :, :] + T[0:32, :]
-        GX[1, :, :] = GX[1, :, :] + T[32:64, :]
-        FB[0:32, :] = FA[0:32, :] + T[64:96, :]
-        FB[33 * 32 : 34 * 32, :] = FA[33 * 32 : 34 * 32, :] + T[96:128, :]
-
-        def correct(y, _):
-            at = pl.ds(pl.multiple_of(y * 32 + 32, 32), 32)
-            FB[at, :] = keep32 * (FA[at, :] + PC[pl.ds(pl.multiple_of((y >> 1) * 32, 32), 32), :])
+            double(PC, (y + 1) * 32, pick(P0[at : at + 16, :], index_p))
+        coarse_z(P0)
+        CB[0:16, :] = pick(outer(P0, 0), index_p)
+        CB[16:32, :] = pick(outer(P0, 1), index_p)
+        double(PC, 0, pick(outer(P0, 2), index_p))
+        double(PC, 17 * 32, pick(outer(P0, 3), index_p))
+
+        def last_sweep(y, _):
+            at = pl.multiple_of(y * 32, 32)
+            center = PC[pl.ds(at + 32, 32), :]
+            low = jnp.broadcast_to(CB[pl.ds(y, 1), :], (32, 128))
+            high = jnp.broadcast_to(CB[pl.ds(y + 16, 1), :], (32, 128))
+            around = jnp.where(first32 > 0, low, roll(center, 1, 0)) + jnp.where(last32 > 0, high, roll(center, -1, 0))
+            around = around + (pick(center, index_low) * mask_low32 + pick(center, index_high) * mask_high32)
+            around = around + (CGZ[pl.ds(at, 32), :] + center)
+            shared = center * (1.0 / 3.0) + around * (1.0 / 9.0)
+
+            def one(k, beside):
+                rows_k = pl.ds(pl.multiple_of(y * 64 + k * 32 + 32, 32), 32)
+                new = FB[rows_k, :] + keep32 * (shared + PC[pl.ds(beside, 32), :] * (1.0 / 9.0))
+                FA[rows_k, :] = new
+                return new
+
+            T[pl.ds(at, 32), :] = one(0, at) + one(1, pl.multiple_of(at + 64, 32))
             return 0
 
-        lax.fori_loop(0, 32, correct, 0, unroll=4)
-
-        def last_sweep(y, _):
-            def one(k):
-                at = pl.multiple_of(k * 32, 32)
-                center = FB[pl.ds(at + 32, 32), :]
-                around = fine_around(FB, k, center)
-                new = keep32 * (G[pl.ds(at, 32), :] + center * (1.0 / 3.0) + around * (1.0 / 9.0))
-                FA[pl.ds(at + 32, 32), :] = new
-                return new
-
-            both = one(2 * y) + one(2 * y + 1)
-            T[pl.ds(pl.multiple_of(y * 32, 32), 32), :] = both
-            return 0
-
-        lax.fori_loop(0, 16, last_sweep, 0)
+        lax.fori_loop(0, 16, last_sweep, 0, unroll=4)
         for y in range(16):
             t = T[pl.ds(y * 32, 16, stride=2), :] + T[pl.ds(y * 32 + 1, 16, stride=2), :]
             means = pick(t + roll(t, -1, 1), index_in) * 0.125
@@ -666,7 +688,7 @@
                 rows(34 * 32),
                 rows(32 * 32),
                 rows(32 * 32),
-                rows(16 * 32),
+                rows(18 * 32),
                 rows(16 * 32),
                 rows(16 * 32),
                 rows(2, 32),
@@ -690,8 +712,8 @@
                 rows(64),
                 rows(16),
                 rows(8),
-                rows(4, 40),
-                rows(8, 40),
+                rows(4, 24),
+                rows(8, 24),
                 rows(4, 48),
                 rows(4, 48),
                 rows(2, 4, 32),
@@ -700,8 +722,8 @@
                 rows(2, 4, 8),
                 rows(2, 4, 32),
                 rows(2, 4, 8),
-                rows(2, 4, 40),
-                rows(2, 8, 40),
+                rows(2, 4, 24),
+                rows(2, 8, 24),
                 rows(2, 8),
                 rows(2, 7, 8),
                 rows(2, 8),

time: 61.4 us -> 58.9 us (0.959)
  Pallas kernels: 58.5 us -> 56 us
    pallas_call x1, Pallas kernels: 58.5 us -> 56 us  [local(): pl.pallas_call(lambda *refs: kernel(nx, ny, *refs), out_shape=(jax.ShapeD...]
where the time goes in v3:
time: 58.9 us; the launch traced here: 58.7 us
  Pallas kernels  56 us (95%)
  local copies, waits for them, and re-layouts  1.45 us (2%)
  between operations  1.29 us (2%)
    pallas_call x1, Pallas kernels, local(): pl.pallas_call(lambda *refs: kernel(nx, ny, *refs), out_shape=(jax.ShapeD...  56 us
    unnamed x2, local copies, waits for them, and re-layouts  1.45 us

profile of v3, /device:TPU:1, one launch (start us, length us, event | category | flops | bytes accessed | tf_op | source)
XLA Modules:
  0.0 58.7 jit_solution(3888357395395870403)
XLA Ops:
  1.3 56.0 %vcycles.1 = (f32[1,1,4,32,1024]{4,3,2,1,0:T(8,128)S(1)}, f32[256,128]{1,0:T(8,128)S(1)}) custom-call(s32[1,1,4]{2,1,0:T(1,128)} %refs_0_.1, s32[1,1,4,6]{3,2,1,0:T(4,128)} %refs_1_.1, s32[1,1]{1,0:T(1,128)S(6)} %copy.11.refs_2_, f32[1,1,4,32,1024]{4,3,2,1,0:T(8,128)} %refs_3_.1, f32[1,1,4,32,1024]{4,3,2,1,0:T(8,128)} %refs_4_.1, f32[256,128]{1,0:T(8,128)} %bitcast.4, ...), custom_call_target="tpu_custom_call" | custom-call | tf_op jit(solution)/shard_map/vcycles/pallas_call | solution.py:673
  57.3 0.8 %copy.12 = f32[1,1,4,32,1024]{4,3,2,1,0:T(8,128)} copy(f32[1,1,4,32,1024]{4,3,2,1,0:T(8,128)S(1)} %get-tuple-element.8) | data formatting | bytes 1048576
  58.1 0.7 %copy.13 = f32[16,16,128]{2,1,0:T(8,128)} copy(f32[16,16,128]{2,1,0:T(8,128)S(1)} %bitcast.3) | data formatting | bytes 262144
